TPU v7x, 128 devices: a whole 4x4x4 slice. The times are simulated.
128 devices in a mesh: modes: 16 (over z_lo, y, core), tiles: 8 (over z_hi, x).
Axes of the slice: x: 4, y: 4, z: 4 (z_hi: 2, z_lo: 2; z = z_hi * 2 + z_lo), core: 2. Of those that a mesh axis runs over, the one named last changes fastest.
Arguments:
- solution_modes: float32 [512, 32, 8, 128], P('modes', 'tiles'), may hold values from -6 to 6
- coefficient_modes: float32 [128, 32, 8, 128], P('modes', 'tiles'), may hold values from 0.5 to 4
- coupling: float32 [16, 32, 32, 32], P('modes'), may hold values from -0.03125 to 0.03125
- source_block: int32 [16, 32], P('modes'), may hold values from 0 to 15
- expansion_index: int32 [16, 32], P('modes'), may hold values from 0 to 127
Outputs:
- applied: float32 [512, 32, 8, 128], P('modes', 'tiles')
All inputs are finite; a program needn't handle non-finite values.
Results may differ from a plain program's by a relative error of at most 0.0003.
Values sent between devices are 32-bit elements; how exact they have to be, the bound alone decides.
A program may use at most 128 MiB of HBM per device.

v0:
```python
import jax
import jax.numpy as jnp
from jax import lax
from jax.sharding import PartitionSpec as P


def with_halo(value, sides, width):
    for axis, dim in sides:
        count, length = (lax.axis_size(axis), value.shape[dim])
        up = [(i, (i + 1) % count) for i in range(count - 1)]
        down = [(j, i) for i, j in up]
        last = lax.slice_in_dim(value, length - width, length, axis=dim)
        initial = lax.slice_in_dim(value, 0, width, axis=dim)
        before = lax.ppermute(last, axis, up)
        after = lax.ppermute(initial, axis, down)
        value = jnp.concatenate([before, value, after], axis=dim)
    return value


def face_means(coefficient):
    along_first = 0.5 * (coefficient[:, :-1, 1:-1, 1:-1] + coefficient[:, 1:, 1:-1, 1:-1])
    along_second = 0.5 * (coefficient[:, 1:-1, :-1, 1:-1] + coefficient[:, 1:-1, 1:, 1:-1])
    along_third = 0.5 * (coefficient[:, 1:-1, 1:-1, :-1] + coefficient[:, 1:-1, 1:-1, 1:])
    return (along_first, along_second, along_third)


def divergence(blended, along_first, along_second, along_third):
    flux_first = along_first * (blended[:, :-1, 1:-1, 1:-1] - blended[:, 1:, 1:-1, 1:-1])
    flux_second = along_second * (blended[:, 1:-1, :-1, 1:-1] - blended[:, 1:-1, 1:, 1:-1])
    flux_third = along_third * (blended[:, 1:-1, 1:-1, :-1] - blended[:, 1:-1, 1:-1, 1:])
    result = flux_first[:, 1:] - flux_first[:, :-1]
    result = result + flux_second[:, :, 1:] - flux_second[:, :, :-1]
    return result + flux_third[:, :, :, 1:] - flux_third[:, :, :, :-1]


def slot_term(padded_u, faces, block_matrix, offset, expansion, width):
    first_faces, second_faces, third_faces = faces
    source_modes = lax.dynamic_slice_in_dim(padded_u, offset * width, width, 0)
    blended = jnp.einsum(
        "ij,jxyz->ixyz", block_matrix, source_modes, precision=lax.Precision.HIGHEST
    )
    return divergence(
        blended,
        lax.dynamic_index_in_dim(first_faces, expansion, 0, keepdims=False),
        lax.dynamic_index_in_dim(second_faces, expansion, 0, keepdims=False),
        lax.dynamic_index_in_dim(third_faces, expansion, 0, keepdims=False),
    )


def block_output(padded_u, faces, coupling_rows, source_rows, expansion_rows, width):
    shape = (width, padded_u.shape[1] - 2, padded_u.shape[2] - 2, padded_u.shape[3] - 2)

    def advance(running, slot_index):
        source = source_rows[slot_index]
        expansion = expansion_rows[slot_index]
        term = slot_term(padded_u, faces, coupling_rows[slot_index], source, expansion, width)
        return (running + term, None)

    start = jnp.zeros(shape, jnp.float32)
    total, _ = lax.scan(advance, start, jnp.arange(source_rows.shape[0], dtype=jnp.int32))
    return total


def on_device(solution_modes, coefficient_modes, coupling, source_block, expansion_index):
    local_solution = solution_modes.shape[0]
    local_coefficient = coefficient_modes.shape[0]
    width = coupling.shape[2]
    groups = lax.axis_size("modes")
    padding = ((0, 0), (0, 0), (1, 1), (1, 1))
    stacked = jnp.concatenate([solution_modes, coefficient_modes], axis=0)
    rimmed = with_halo(stacked, (("tiles", 1),), 1)
    everyone = lax.all_gather(rimmed, "modes", axis=0, tiled=True)
    trailing = everyone.shape[1:]
    shaped = everyone.reshape((groups, local_solution + local_coefficient) + trailing)
    all_solution = shaped[:, :local_solution].reshape((groups * local_solution,) + trailing)
    all_coefficient = shaped[:, local_solution:].reshape((groups * local_coefficient,) + trailing)
    padded_u = jnp.pad(all_solution, padding)
    padded_a = jnp.pad(all_coefficient, padding)
    faces = face_means(padded_a)
    outputs = block_output(padded_u, faces, coupling[0], source_block[0], expansion_index[0], width)
    return outputs


def solution(mesh):
    placed = (
        P("modes", "tiles", None, None),
        P("modes", "tiles", None, None),
        P("modes", None, None, None),
        P("modes", None),
        P("modes", None),
    )
    return jax.shard_map(
        on_device,
        mesh=mesh,
        in_specs=placed,
        out_specs=P("modes", "tiles", None, None),
        check_vma=False,
    )
```

profile of v0, /device:TPU:7, one launch (start us, length us, event | category | flops | bytes accessed | tf_op | source)
XLA Modules:
  0.0 698.6 jit_solution(3090703868489263197)
XLA Ops:
  11.0 6.4 collective-permute-start
  21.1 91.4 %all-gather.2.cloned.1.call-done = f32[640,6,8,128]{3,2,1,0:T(8,128)} async-done(((f32[40,6,8,128]{3,2,1,0:T(8,128)}), f32[640,6,8,128]{3,2,1,0:T(8,128)}) %all-gather.2.cloned.1.call-update) | async-done | bytes 15728656 | tf_op jit(solution)/shard_map/all_gather | solution.py:72
  114.7 10.5 %slice.107 = f32[16,32,6,8,128]{4,3,2,1,0:T(8,128)} slice(f32[16,40,6,8,128]{4,3,2,1,0:T(8,128)} %bitcast.41), slice={[0:16], [0:32], [0:6], [0:8], [0:128]} | slice | bytes 25165824 | tf_op jit(solution)/shard_map/slice | solution.py:75
  127.0 2.7 fusion.10
  129.7 3.1 fusion.12
  132.8 13.2 %copy.8 = f32[16,32,6,8,128]{4,1,0,3,2:T(8,128)} copy(f32[16,32,6,8,128]{4,3,2,1,0:T(8,128)} %slice.107) | data formatting | bytes 25165824 | tf_op jit(solution)/shard_map/slice | solution.py:75
  146.1 15.0 %pad.8 = f32[512,6,10,130]{3,0,2,1:T(8,128)} pad(f32[512,6,8,128]{3,0,2,1:T(8,128)} %bitcast.39, f32[]{:T(128)} %constant.32.clone.1), padding=0_0x0_0x1_1x1_1 | pad | bytes 28557316 | tf_op jit(solution)/shard_map/jit(_pad)/pad | solution.py:77
  161.1 528.5 %while.11 = (s32[]{:T(128)}, f32[32,4,8,128]{3,0,2,1:T(8,128)}, s32[32]{0:T(128)S(1)}, s32[32]{0:T(128)S(1)}, f32[128,5,8,128]{3,2,1,0:T(8,128)}, /*index=5*/f32...) while((s32[]{:T(128)}, f32[32,4,8,128]{3,0,2,1:T(8,128)}, ...), condition=%wide.region_1.2_spmd.clone, body=%wide.region_0.1_spmd.clone.sunk | while | flops 97650696 | bytes 12662481 | solution.py:60
  164.8 3.3 fusion.24
  181.2 3.3 fusion.24
  191.4 2.6 fusion.28
  197.7 3.3 fusion.24
  207.9 2.6 fusion.28
  214.2 3.3 fusion.24
  224.4 2.6 fusion.28
  230.8 3.3 fusion.24
  240.9 2.6 fusion.28
  247.3 3.3 fusion.24
  257.4 2.6 fusion.28
  263.8 3.3 fusion.24
  274.0 2.6 fusion.28
  280.3 3.3 fusion.24
  290.5 2.6 fusion.28
  296.8 3.3 fusion.24
  307.0 2.6 fusion.28
  313.3 3.3 fusion.24
  323.5 2.6 fusion.28
  329.9 3.3 fusion.24
  346.4 3.3 fusion.24
  356.6 2.6 fusion.28
  362.9 3.3 fusion.24
  373.1 2.6 fusion.28
  379.4 3.3 fusion.24
  395.9 3.3 fusion.24
  406.1 2.6 fusion.28
  412.5 3.3 fusion.24
  422.6 2.6 fusion.28
  429.0 3.3 fusion.24
  445.5 3.3 fusion.24
  455.7 2.6 fusion.28
  462.0 3.3 fusion.24
  472.2 2.6 fusion.28
  478.5 3.3 fusion.24
  488.7 2.6 fusion.28
  495.0 3.3 fusion.24
  511.6 3.3 fusion.24
  528.1 3.3 fusion.24
  544.6 3.3 fusion.24
  554.8 2.6 fusion.28
  561.1 3.3 fusion.24
  571.3 2.6 fusion.28
  577.6 3.3 fusion.24
  587.8 2.6 fusion.28
  594.2 3.3 fusion.24
  604.3 2.6 fusion.28
  610.7 3.3 fusion.24
  627.2 3.3 fusion.24
  637.4 2.6 fusion.28
  643.7 3.3 fusion.24
  653.9 2.6 fusion.28
  660.2 3.3 fusion.24
  670.4 2.6 fusion.28
  676.7 3.3 fusion.24
  686.9 2.6 fusion.28
  (314 shorter events, 235.0 us)
Async XLA Ops:
  6.5 106.0 %all-gather.2.cloned.1.call-start = ((), (), s32[]{:S(2)}) async-start(), calls=%async_computation | async-start | bytes 16711680 | tf_op jit(solution)/shard_map/all_gather | solution.py:72
  8.6 10.6 %collective-permute-start.1 = (f32[40,1,8,128]{3,2,1,0:T(8,128)S(1)}, f32[40,1,8,128]{3,2,1,0:T(8,128)S(1)}, u32[]{:S(2)}, u32[]{:S(2)}) collective-permute-start(f32[40,1,8,128]{3,2,1,0:T(8,128)S(1)} %get-tuple-element.112), channel_id=1, source_target_pairs={{1,0},{2,1},{3,2},{4,3},{5,4},{6,5},{7,6},{9,8},{10,9},{11,10},{12... | collective-permute-start | bytes 491528 | tf_op jit(solution)/shard_map/ppermute | solution.py:15
  11.0 9.0 %collective-permute-start = (f32[40,1,8,128]{3,2,1,0:T(8,128)S(1)}, f32[40,1,8,128]{3,2,1,0:T(8,128)S(1)}, u32[]{:S(2)}, u32[]{:S(2)}) collective-permute-start(f32[40,1,8,128]{3,2,1,0:T(8,128)S(1)} %get-tuple-element.111), channel_id=1, source_target_pairs={{0,1},{1,2},{2,3},{3,4},{4,5},{5,6},{6,7},{8,9},{9,10},{10,11},{11... | collective-permute-start | bytes 491528 | tf_op jit(solution)/shard_map/ppermute | solution.py:14
  146.0 15.0 %copy-start = (s32[1,32]{1,0:T(1,128)S(1)}, s32[1,32]{1,0:T(1,128)}, u32[]{:S(2)}) copy-start(s32[1,32]{1,0:T(1,128)} %param.11) | copy-start | bytes 388
  146.0 15.0 %copy-start.1 = (s32[1,32]{1,0:T(1,128)S(1)}, s32[1,32]{1,0:T(1,128)}, u32[]{:S(2)}) copy-start(s32[1,32]{1,0:T(1,128)} %param.10) | copy-start | bytes 388
Sparse Core Ops, SparseCore 0:
  21.2 91.2 all-gather.1
where the time goes:
time: 710 us; the launch traced here: 699 us
  local copies, waits for them, and re-layouts  177 us (25%)
  other arithmetic  161 us (23%)
  loops' own time  138 us (19%)
  matrix products  106 us (15%)
  waiting for transfers between devices  94 us (13%)
  between operations  13.4 us (2%)
  starting transfers between devices  8.9 us (1%)
    another operation x1, loops' own time, block_output(): lax.scan(advance, start, jnp.arange(source_rows.shape[0], dtype=jnp.int32))  138 us
    dot_general x32, matrix products, slot_term(): jnp.einsum('ij,jxyz->ixyz', block_matrix, source_modes, precision=lax.Pre...  106 us
    all_gather x1, waiting for transfers between devices, on_device(): everyone = lax.all_gather(rimmed, 'modes', axis=0, tiled=True)  91.4 us
    add x32, other arithmetic, advance(): return (running + term, None)  84.6 us
    mul x32, other arithmetic, divergence(): along_third * (blended[:, 1:-1, 1:-1, :-1] - blended[:, 1:-1, 1:-1, 1:])  42.9 us
    mul x32, local copies, waits for them, and re-layouts, divergence(): along_third * (blended[:, 1:-1, 1:-1, :-1] - blended[:, 1:-1, 1:-1, 1:])  24.5 us
    mul x32, local copies, waits for them, and re-layouts, divergence(): along_second * (blended[:, 1:-1, :-1, 1:-1] - blended[:, 1:-1, 1:, 1:-1])  24.3 us
    slice x2, local copies, waits for them, and re-layouts, on_device(): shaped[:, :local_solution].reshape((groups * local_solution,) + trailing)  23.7 us
  transfers between devices with their start and end apart: 3, of which 3 were waited for; matrix products, arithmetic and copies ran while one was open for 0% of the time, Pallas kernels for 0%

commit v1 on v0

v1 whole, which is shorter than its diff:
```python
import functools

import jax
import jax.numpy as jnp
from jax import lax
from jax.experimental import pallas as pl
from jax.experimental.pallas import tpu as pltpu
from jax.sharding import PartitionSpec as P

F32, BF16 = jnp.float32, jnp.bfloat16


def lanes(shape):
    return lax.broadcasted_iota(jnp.int32, shape, len(shape) - 1)


def face_tiles(roll, comb, x0, x1, zh, xm, xp):
    lane = lanes(x0.shape)
    zz, yy, low = lane % 8, (lane // 8) % 8, lane < 64
    zero = jnp.zeros_like(x0)
    r0, r1, rp, rm = (roll(v, 64) for v in (x0, x1, xp, xm))
    fx0 = comb(x0, jnp.where(low, r0, r1))
    fx1 = comb(x1, jnp.where(low, r1, rp))
    fy0 = comb(x0, jnp.where(yy < 7, roll(x0, 120), zero))
    fy1 = comb(x1, jnp.where(yy < 7, roll(x1, 120), zero))
    fz0 = comb(x0, jnp.where(zz < 7, roll(x0, 127), zh))
    fz1 = comb(x1, jnp.where(zz < 7, roll(x1, 127), roll(zh, 1)))
    group = lane // 8
    edge = jnp.where(group == 8, r0, jnp.where(group == 9, roll(x0, 8),
                     jnp.where(group == 10, roll(x1, 80), roll(x1, 24))))
    edge = jnp.where(group < 12, edge, zero)
    t6 = comb(jnp.where(low, rm, zero), jnp.where(low, x0, edge))
    t7 = comb(zh, jnp.where(zz == 0, x0, roll(x1, 1)))
    t7 = jnp.where(zz < 2, t7, zero)
    return fx0, fx1, fy0, fy1, fz0, fz1, t6, t7


def divergence_tiles(roll, fx0, fx1, fy0, fy1, fz0, fz1, t6, t7):
    lane = lanes(fx0.shape)
    zz, yy, low = lane % 8, (lane // 8) % 8, lane < 64
    rx0, rx1 = roll(fx0, 64), roll(fx1, 64)
    ly0 = jnp.where(low, roll(t6, 64), roll(t6, 120))
    ly1 = jnp.where(low, roll(t6, 48), roll(t6, 104))
    out0 = (fx0 - jnp.where(low, t6, rx0)) + (fy0 - jnp.where(yy == 0, ly0, roll(fy0, 8)))
    out0 = out0 + (fz0 - jnp.where(zz == 0, t7, roll(fz0, 1)))
    out1 = (fx1 - jnp.where(low, rx0, rx1)) + (fy1 - jnp.where(yy == 0, ly1, roll(fy1, 8)))
    out1 = out1 + (fz1 - jnp.where(zz == 0, roll(t7, 127), roll(fz1, 1)))
    return out0, out1


def difference(own, other):
    return own - other


def mean(own, other):
    return 0.5 * (own + other)


def xroll(value, shift):
    return jnp.roll(value, shift, axis=-1)


def kroll(value, shift):
    return pltpu.roll(value, shift, value.ndim - 1)


def slots_kernel(sb_ref, ei_ref, c_ref, d_ref, a_ref, out_ref):
    block = pl.program_id(0)
    slots = c_ref.shape[1]
    rows = c_ref.shape[2]
    width = d_ref.shape[2]

    def advance(s, total):
        j = sb_ref[block * slots + s]
        k = ei_ref[block * slots + s]
        v = jnp.dot(c_ref[0, s], d_ref[j], preferred_element_type=F32)
        return total + v.reshape(rows // 8, 8, width) * a_ref[k][None]

    total = lax.fori_loop(0, slots, advance, jnp.zeros((rows // 8, 8, width), F32))
    total = total.reshape(rows, width)
    tiles = [total[:, 128 * t:128 * (t + 1)] for t in range(8)]
    out0, out1 = divergence_tiles(kroll, *tiles)
    out_ref[0, 0] = out0
    out_ref[0, 1] = out1


def slots_call(sb, ei, cext, dext, abar):
    blocks, slots, rows, depth = cext.shape
    return pl.pallas_call(
        slots_kernel,
        out_shape=jax.ShapeDtypeStruct((blocks, 2, rows, 128), F32),
        grid_spec=pltpu.PrefetchScalarGridSpec(
            num_scalar_prefetch=2,
            grid=(blocks,),
            in_specs=[
                pl.BlockSpec((1, slots, rows, depth), lambda b, *_: (b, 0, 0, 0)),
                pl.BlockSpec(memory_space=pltpu.VMEM),
                pl.BlockSpec(memory_space=pltpu.VMEM),
            ],
            out_specs=pl.BlockSpec((1, 2, rows, 128), lambda b, *_: (b, 0, 0, 0)),
        ),
        compiler_params=pltpu.CompilerParams(vmem_limit_bytes=60 << 20),
        name="slots",
    )(sb, ei, cext, dext, abar)


def high_low(value):
    high = lax.reduce_precision(value, 8, 7)
    return high.astype(BF16), (value - high).astype(BF16)


def pieces_of(stacked):
    rows = stacked.shape[0]
    split = stacked.reshape(rows, 2, 2, 8, 16, 8).transpose(4, 1, 0, 2, 3, 5)
    center = split.reshape(16, 2, rows, 128)
    above = jnp.pad(center[1:], ((0, 1), (0, 0), (0, 0), (0, 0)))
    below = jnp.pad(center[:-1], ((1, 0), (0, 0), (0, 0), (0, 0)))
    zz = lanes((16, rows, 128)) % 8
    halo = jnp.where(zz == 7, xroll(above[:, 0], 7), 0.0)
    halo = jnp.where(zz == 6, xroll(above[:, 1], 6), halo)
    halo = jnp.where(zz == 0, xroll(below[:, 0], 121), halo)
    halo = jnp.where(zz == 1, xroll(below[:, 1], 122), halo)
    return jnp.concatenate([center, halo[:, None]], axis=1)


def on_device(solution_modes, coefficient_modes, coupling, source_block, expansion_index):
    nu, na = solution_modes.shape[0], coefficient_modes.shape[0]
    stacked = jnp.concatenate([solution_modes, coefficient_modes], axis=0)
    pieces = pieces_of(stacked)
    got = lax.all_to_all(pieces, "modes", 0, 0, tiled=True)
    tiles = lax.axis_size("tiles")
    up = [(i, i + 1) for i in range(tiles - 1)]
    xm = lax.ppermute(got[:, 1], "tiles", up)
    xp = lax.ppermute(got[:, 0], "tiles", [(j, i) for i, j in up])
    parts = (got[:, 0], got[:, 1], got[:, 2], xm, xp)
    delta = jnp.concatenate(face_tiles(xroll, difference, *(v[:, :nu] for v in parts)), axis=-1)
    abar = jnp.concatenate(face_tiles(xroll, mean, *(v[:, nu:] for v in parts)), axis=-1)
    abar = abar.reshape(16 * na, 1, 1024)
    abar = jnp.broadcast_to(abar, (16 * na, 8, 1024))
    dh, dl = high_low(delta)
    dext = jnp.concatenate([dh, dl, dh], axis=1)
    everyone = lax.all_gather(coupling[0], "modes", axis=0)
    ch, cl = high_low(everyone)
    cext = jnp.concatenate([ch, ch, cl], axis=-1)
    sb = lax.all_gather(source_block[0], "modes", axis=0).reshape(-1)
    ei = lax.all_gather(expansion_index[0], "modes", axis=0).reshape(-1)
    out = slots_call(sb, ei, cext, dext, abar)
    back = lax.all_to_all(out, "modes", 0, 0, tiled=True)
    back = back.reshape(16, 2, nu, 2, 8, 8).transpose(2, 1, 3, 4, 0, 5)
    return back.reshape(solution_modes.shape)


def solution(mesh):
    placed = (
        P("modes", "tiles", None, None),
        P("modes", "tiles", None, None),
        P("modes", None, None, None),
        P("modes", None),
        P("modes", None),
    )
    return jax.shard_map(
        on_device,
        mesh=mesh,
        in_specs=placed,
        out_specs=P("modes", "tiles", None, None),
        check_vma=False,
    )
```

time: 710 us -> 237 us (0.33); the launches traced: 699 us -> 233 us
  local copies, waits for them, and re-layouts: 177 us -> 30.7 us
  other arithmetic: 161 us -> 20.6 us
  loops' own time: 138 us -> 0 us
  matrix products: 106 us -> 0 us
  Pallas kernels: 0 us -> 90.9 us
  waiting for transfers between devices: 94 us -> 4.75 us
  blocking collectives: 0 us -> 56.9 us
    another operation x1 -> x0, loops' own time: 138 us -> none  [block_output(): lax.scan(advance, start, jnp.arange(source_rows.shape[0], dtype=jnp.int32))]
    dot_general x32 -> x0, matrix products: 106 us -> none  [slot_term(): jnp.einsum('ij,jxyz->ixyz', block_matrix, source_modes, precision=lax.Pre...]
    all_gather x1, waiting for transfers between devices: 91.4 us -> 0.02 us  [on_device(): everyone = lax.all_gather(coupling[0], 'modes', axis=0)]
    pallas_call x0 -> x1, Pallas kernels: none -> 90.9 us  [slots_call(): pl.pallas_call(slots_kernel, out_shape=jax.ShapeDtypeStruct((blocks, 2, r...]
    add x32 -> x0, other arithmetic: 84.6 us -> none  [advance(): return (running + term, None)]
    mul x99 -> x0, other arithmetic: 75.5 us -> none  [the longest x32 42.9 us: divergence(): along_third * (blended[:, 1:-1, 1:-1, :-1] - blended[:, 1:-1, 1:-1, 1:])]
    mul x96 -> x0, local copies, waits for them, and re-layouts: 72.4 us -> none  [the longest x32 24.5 us: divergence(): along_third * (blended[:, 1:-1, 1:-1, :-1] - blended[:, 1:-1, 1:-1, 1:])]
    dynamic_slice x96 -> x0, local copies, waits for them, and re-layouts: 59.4 us -> none  [the longest x32 19.9 us: advance(): expansion = expansion_rows[slot_index]]
  transfers between devices with their start and end apart: 3 -> 4, of which waited for: 3 -> 1; matrix products, arithmetic and copies ran while one was open for 0% -> 5% of each run, Pallas kernels for 0% -> 0%
where the time goes in v1:
time: 237 us; the launch traced here: 233 us
  Pallas kernels  90.9 us (38%)
  blocking collectives  56.9 us (24%)
  local copies, waits for them, and re-layouts  30.7 us (13%)
  other arithmetic  20.6 us (9%)
  starting transfers between devices  15.6 us (7%)
  between operations  13.9 us (6%)
  waiting for transfers between devices  4.75 us (2%)
    pallas_call x1, Pallas kernels, slots_call(): pl.pallas_call(slots_kernel, out_shape=jax.ShapeDtypeStruct((blocks, 2, r...  90.9 us
    all_gather x1, blocking collectives, on_device(): sb = lax.all_gather(source_block[0], 'modes', axis=0).reshape(-1)  25.5 us
    all_gather x1, blocking collectives, on_device(): ei = lax.all_gather(expansion_index[0], 'modes', axis=0).reshape(-1)  17.3 us
    all_to_all x1, blocking collectives, on_device(): back = lax.all_to_all(out, 'modes', 0, 0, tiled=True)  14.1 us
    concatenate x16, local copies, waits for them, and re-layouts, xroll(): return jnp.roll(value, shift, axis=-1)  12.8 us
    ppermute x1, starting transfers between devices, on_device(): xm = lax.ppermute(got[:, 1], 'tiles', up)  6.62 us
    all_to_all x1, starting transfers between devices, on_device(): got = lax.all_to_all(pieces, 'modes', 0, 0, tiled=True)  6.51 us
    convert_element_type x2, other arithmetic, high_low(): return (high.astype(BF16), (value - high).astype(BF16))  5.96 us
  transfers between devices with their start and end apart: 4, of which 1 were waited for; matrix products, arithmetic and copies ran while one was open for 5% of the time, Pallas kernels for 0%

profile of v1, /device:TPU:7, one launch (start us, length us, event | category | flops | bytes accessed | tf_op | source)
XLA Modules:
  0.0 233.4 jit_solution(11941286216896210373)
XLA Ops:
  6.5 1.2 pad_maximum_fusion.3
  7.7 0.6 copy.36
  8.4 1.6 copy.37
  10.0 0.3 fusion.57
  10.3 0.2 copy.43
  10.6 0.3 fusion.5
  11.0 0.6 slice_bitcast_fusion.8
  11.6 1.1 slice_bitcast_fusion.1
  12.7 0.2 copy.38
  13.0 0.3 fusion.3
  13.3 0.6 slice_bitcast_fusion.9
  13.9 1.1 slice_bitcast_fusion.2
  15.0 0.6 slice_bitcast_fusion.10
  15.6 1.1 slice_bitcast_fusion.3
  16.7 1.4 copy.48
  18.1 1.1 copy.47
  19.2 0.1 copy-done.1
  19.3 1.1 copy.45
  20.4 1.0 copy.44
  21.4 0.2 copy.46
  21.6 1.1 copy.41
  22.7 1.1 copy.39
  23.7 1.1 copy.40
  24.8 1.0 copy.42
  25.8 1.6 maximum_select_fusion
  27.5 1.1 pad_maximum_fusion.2
  28.5 6.5 %all-to-all-start = ((f32[16,3,40,128]{3,2,1,0:T(8,128)}), f32[16,3,40,128]{3,2,1,0:T(8,128)S(1)}, u32[]{:S(2)}, u32[]{:S(2)}) async-start(f32[16,3,40,128]{3,2,1,0:T(8,128)} %pad_maximum_fusion.2), calls=%async_computation | async-start | bytes 1966080 | tf_op jit(solution)/shard_map/all_to_all | solution.py:130
  35.1 0.7 all-gather.4.cloned.1.call-update
  35.8 25.5 %all-gather = s32[16,1,32]{2,1,0:T(1,128)S(1)} all-gather(s32[1,1,32]{2,1,0:T(1,128)S(1)} %bitcast.57), channel_id=1, replica_groups=mesh['modes'=16,'tiles'=8] {'modes'}, dimensions={0}, use_global_device_ids=true | all-gather | bytes 2176 | tf_op jit(solution)/shard_map/all_gather | solution.py:145
  61.3 0.5 broadcast.189
  61.8 0.7 reduce.6
  62.5 0.7 reshape.153.sb_ref
  63.1 17.3 %all-gather.1 = s32[16,1,32]{2,1,0:T(1,128)S(1)} all-gather(s32[1,1,32]{2,1,0:T(1,128)S(1)} %bitcast.58), channel_id=1, replica_groups=mesh['modes'=16,'tiles'=8] {'modes'}, dimensions={0}, use_global_device_ids=true | all-gather | bytes 2176 | tf_op jit(solution)/shard_map/all_gather | solution.py:146
  80.5 0.7 reduce.7
  81.2 0.7 reshape.154.ei_ref
  83.4 2.5 %collective-permute-start = (f32[16,40,128]{2,1,0:T(8,128)S(1)}, f32[16,40,128]{2,1,0:T(8,128)S(1)}, u32[]{:S(2)}, u32[]{:S(2)}) collective-permute-start(f32[16,40,128]{2,1,0:T(8,128)S(1)} %get-tuple-element.17), channel_id=1, source_target_pairs={{1,0},{2,1},{3,2},{4,3},{5,4},{6,5},{7,6},{9,8},{10,9},{11,10},{12... | collective-permute-start | bytes 983048 | tf_op jit(solution)/shard_map/ppermute | solution.py:134
  85.9 6.6 %collective-permute-start.1 = (f32[16,40,128]{2,1,0:T(8,128)S(1)}, f32[16,40,128]{2,1,0:T(8,128)S(1)}, u32[]{:S(2)}, u32[]{:S(2)}) collective-permute-start(f32[16,40,128]{2,1,0:T(8,128)S(1)} %get-tuple-element.16), channel_id=1, source_target_pairs={{0,1},{1,2},{2,3},{3,4},{4,5},{5,6},{6,7},{8,9},{9,10},{10,11},{11... | collective-permute-start | bytes 983048 | tf_op jit(solution)/shard_map/ppermute | solution.py:133
  92.5 0.1 fusion.69
  92.6 0.1 fusion.68
  92.8 0.1 fusion.72
  92.9 0.1 fusion.67
  93.1 0.1 fusion.73
  93.3 0.2 subtract_dynamic-update-slice_fusion
  93.9 0.1 fusion.66
  94.0 4.0 %collective-permute-done = f32[16,40,128]{2,1,0:T(8,128)S(1)} collective-permute-done((f32[16,40,128]{2,1,0:T(8,128)S(1)}, f32[16,40,128]{2,1,0:T(8,128)S(1)}, u32[]{:S(2)}, u32[]{:S(2)}) %collective-permute-start) | collective-permute-done | bytes 327712 | tf_op jit(solution)/shard_map/ppermute | solution.py:134
  98.2 0.2 fusion.15
  98.4 0.1 fusion.17
  98.6 0.1 fusion.19
  98.7 0.1 fusion.9
  98.9 0.2 fusion.11
  99.1 0.1 fusion.70
  99.2 0.4 fusion.21
  99.7 0.1 fusion.27
  99.8 0.4 fusion.1
  100.3 1.8 pad_maximum_fusion.1.d_ref
  102.7 0.2 fusion.49
  103.0 5.5 %reduce-precision_convert_fusion = (bf16[16,32,32,32]{3,2,1,0:T(8,128)(2,1)S(1)}, bf16[16,32,32,32]{3,2,1,0:T(8,128)(2,1)S(1)}) fusion(f32[16,32,32,32]{3,2,1,0:T(8,128)} %all-gather.4.cloned.1.call-done), kind=kLoop, calls=%fused_computation.1 | loop fusion | flops 2097152 | bytes 4194304 | tf_op jit(solution)/shard_map/convert_element_type | solution.py:109
  108.6 5.2 %pad_maximum_fusion.c_ref = bf16[16,32,32,96]{3,2,1,0:T(8,128)(2,1)} fusion(bf16[16,32,32,32]{3,2,1,0:T(8,128)(2,1)S(1)} %get-tuple-element.6, bf16[16,32,32,32]{3,2,1,0:T(8,128)(2,1)S(1)} %get-tuple-element.5), kind=kLoop, calls=%fused_computation.3 | loop fusion | flops 9437184 | bytes 5242880 | tf_op jit(solution)/shard_map/concatenate | solution.py:144
  113.7 2.5 %broadcast_in_dim.22.a_ref = f32[128,8,1024]{2,1,0:T(8,128)} broadcast(f32[128,1024]{1,0:T(8,128)S(1)} %bitcast.56), dimensions={0,2} | broadcast | bytes 4718592 | tf_op jit(solution)/shard_map/broadcast_in_dim | solution.py:139
  116.3 90.9 %slots.1 = f32[16,2,32,128]{3,2,1,0:T(8,128)} custom-call(s32[512]{0:T(512)} %reshape.153.sb_ref, s32[512]{0:T(512)} %reshape.154.ei_ref, bf16[16,32,32,96]{3,2,1,0:T(8,128)(2,1)} %pad_maximum_fusion.c_ref, bf16[16,96,1024]{2,1,0:T(8,128)(2,1)} %pad_maximum_fusion.1.d_ref, f32[128,8,1024]{2,1,0:T(8,128)} %broadcast_in_dim.22.a_ref), custom_call_target="tpu_custom_call" | custom-call | tf_op jit(solution)/shard_map/slots/pallas_call | solution.py:89
  207.2 14.1 %all_to_all.10 = f32[16,2,32,128]{3,2,1,0:T(8,128)S(1)} all-to-all(f32[16,2,32,128]{3,2,1,0:T(8,128)} %slots.1), channel_id=1, replica_groups=mesh['modes'=16,'tiles'=8] {'modes'}, dimensions={0} | all-to-all | bytes 1048576 | tf_op jit(solution)/shard_map/all_to_all | solution.py:148
  221.2 0.6 copy.52
  221.9 1.6 copy.53
  223.5 3.0 %copy.54 = f32[32,4,8,128]{3,2,1,0:T(8,128)} copy(f32[32,4,8,128]{0,3,2,1:T(8,128)} %bitcast.52) | data formatting | bytes 1048576 | tf_op jit(solution)/shard_map/reshape | solution.py:150
  (63 shorter events, 3.0 us)
Async XLA Ops:
  13.9 2.8 %copy-start = (f32[16,2,40,2,8,8]{2,5,4,3,1,0:T(8,128)S(1)}, f32[16,2,40,2,8,8]{2,5,4,3,1,0:T(8,128)}, u32[]{:S(2)}) copy-start(f32[16,2,40,2,8,8]{2,5,4,3,1,0:T(8,128)} %copy.37) | copy-start | bytes 1966084
  18.1 1.2 copy-start.1
  18.1 3.5 %copy-start.2 = (f32[16,1,40,121]{2,3,0,1:T(8,128)S(1)}, f32[16,1,40,121]{2,3,0,1:T(8,128)}, u32[]{:S(2)}) copy-start(f32[16,1,40,121]{2,3,0,1:T(8,128)} %slice_bitcast_fusion.2) | copy-start | bytes 929284
  19.3 3.3 %copy-start.3 = (f32[16,1,40,122]{2,3,0,1:T(8,128)S(1)}, f32[16,1,40,122]{2,3,0,1:T(8,128)}, u32[]{:S(2)}) copy-start(f32[16,1,40,122]{2,3,0,1:T(8,128)} %slice_bitcast_fusion.3) | copy-start | bytes 936964
  22.6 3.2 %copy-start.5 = (f32[16,1,40,122]{3,2,1,0:T(8,128)S(1)}, f32[16,1,40,122]{3,2,1,0:T(8,128)}, u32[]{:S(2)}) copy-start(f32[16,1,40,122]{3,2,1,0:T(8,128)} %copy.45) | copy-start | bytes 936964
  23.7 3.7 %copy-start.4 = (f32[16,2,40,128]{3,2,1,0:T(8,128)S(1)}, f32[16,2,40,128]{3,2,1,0:T(8,128)}, u32[]{:S(2)}) copy-start(f32[16,2,40,128]{3,2,1,0:T(8,128)} %copy.48) | copy-start | bytes 1966084
  27.4 8.3 %copy-start.6 = (s32[1,32]{1,0:T(1,128)S(1)}, s32[1,32]{1,0:T(1,128)}, u32[]{:S(2)}) copy-start(s32[1,32]{1,0:T(1,128)} %param.8) | copy-start | bytes 388
  27.4 35.7 %copy-start.7 = (s32[1,32]{1,0:T(1,128)S(1)}, s32[1,32]{1,0:T(1,128)}, u32[]{:S(2)}) copy-start(s32[1,32]{1,0:T(1,128)} %param.9) | copy-start | bytes 388
  28.5 53.3 %all-to-all-start = ((f32[16,3,40,128]{3,2,1,0:T(8,128)}), f32[16,3,40,128]{3,2,1,0:T(8,128)S(1)}, u32[]{:S(2)}, u32[]{:S(2)}) async-start(f32[16,3,40,128]{3,2,1,0:T(8,128)} %pad_maximum_fusion.2), calls=%async_computation | async-start | bytes 1966080 | tf_op jit(solution)/shard_map/all_to_all | solution.py:130
  35.0 68.0 %all-gather.4.cloned.1.call-start = ((), (), s32[]{:S(2)}) async-start(), calls=%async_computation.2 | async-start | bytes 8912896 | tf_op jit(solution)/shard_map/all_gather | solution.py:142
  83.4 14.7 %collective-permute-start = (f32[16,40,128]{2,1,0:T(8,128)S(1)}, f32[16,40,128]{2,1,0:T(8,128)S(1)}, u32[]{:S(2)}, u32[]{:S(2)}) collective-permute-start(f32[16,40,128]{2,1,0:T(8,128)S(1)} %get-tuple-element.17), channel_id=1, source_target_pairs={{1,0},{2,1},{3,2},{4,3},{5,4},{6,5},{7,6},{9,8},{10,9},{11,10},{12... | collective-permute-start | bytes 983048 | tf_op jit(solution)/shard_map/ppermute | solution.py:134
  85.9 13.2 %collective-permute-start.1 = (f32[16,40,128]{2,1,0:T(8,128)S(1)}, f32[16,40,128]{2,1,0:T(8,128)S(1)}, u32[]{:S(2)}, u32[]{:S(2)}) collective-permute-start(f32[16,40,128]{2,1,0:T(8,128)S(1)} %get-tuple-element.16), channel_id=1, source_target_pairs={{0,1},{1,2},{2,3},{3,4},{4,5},{5,6},{6,7},{8,9},{9,10},{10,11},{11... | collective-permute-start | bytes 983048 | tf_op jit(solution)/shard_map/ppermute | solution.py:133
Sparse Core Ops, SparseCore 0:
  37.6 54.1 all-gather.3

commit v2 on v1

v2 whole, which is shorter than its diff:
```python
import functools

import jax
import jax.numpy as jnp
from jax import lax
from jax.experimental import pallas as pl
from jax.experimental.pallas import tpu as pltpu
from jax.sharding import PartitionSpec as P

F32, BF16 = jnp.float32, jnp.bfloat16


def lanes(shape):
    return lax.broadcasted_iota(jnp.int32, shape, len(shape) - 1)


def face_tiles(roll, comb, x0, x1, zh, xm, xp):
    lane = lanes(x0.shape)
    zz, yy, low = lane % 8, (lane // 8) % 8, lane < 64
    zero = jnp.zeros_like(x0)
    r0, r1, rp, rm = (roll(v, 64) for v in (x0, x1, xp, xm))
    yield comb(x0, jnp.where(low, r0, r1))
    yield comb(x1, jnp.where(low, r1, rp))
    yield comb(x0, jnp.where(low, rm, r0))
    yield comb(x1, jnp.where(low, r0, r1))
    for x in (x0, x1):
        yield comb(x, jnp.where(yy < 7, roll(x, 120), zero))
    for x in (x0, x1):
        yield comb(x, jnp.where(yy > 0, roll(x, 8), zero))
    yield comb(x0, jnp.where(zz < 7, roll(x0, 127), zh))
    yield comb(x1, jnp.where(zz < 7, roll(x1, 127), roll(zh, 1)))
    yield comb(x0, jnp.where(zz > 0, roll(x0, 1), zh))
    yield comb(x1, jnp.where(zz > 0, roll(x1, 1), roll(zh, 127)))


def difference(own, other):
    return own - other


def mean(own, other):
    return 0.5 * (own + other)


def xroll(value, shift):
    return jnp.roll(value, shift, axis=-1)


def kroll(value, shift):
    return pltpu.roll(value, shift, value.ndim - 1)


def prepare(got_ref, xm_ref, xp_ref, delta, faces, nu):
    def one(j, carry):
        def tiles(rows):
            return (got_ref[j, 0, rows], got_ref[j, 1, rows], got_ref[j, 2, rows], xm_ref[j, rows], xp_ref[j, rows])

        for m in range(nu // 8):
            rows = pl.ds(8 * m, 8)
            for f, value in enumerate(face_tiles(kroll, difference, *tiles(rows))):
                delta[j, f, rows] = value
        own = pl.ds(pl.multiple_of(8 * j, 8), 8)
        for f, value in enumerate(face_tiles(kroll, mean, *tiles(pl.ds(nu, 8)))):
            faces[f, own] = value
        return carry

    lax.fori_loop(0, got_ref.shape[0], one, 0)


def slots_kernel(nu, sb_ref, ei_ref, c_ref, got_ref, xm_ref, xp_ref, out_ref, delta, faces, wh, wl):
    block = pl.program_id(0)

    @pl.when(block == 0)
    def _():
        prepare(got_ref, xm_ref, xp_ref, delta, faces, nu)

    def chunk(c, total):
        for s in range(8):
            j = sb_ref[block * 32 + c * 8 + s]
            k = ei_ref[block * 32 + c * 8 + s]
            for t in range(2):
                coefficient = [faces[2 * f + t, pl.ds(k, 8, stride=0)] for f in range(6)]
                for m in range(nu // 16):
                    pair = []
                    for h in range(2):
                        rows = pl.ds(16 * m + 8 * h, 8)
                        w = coefficient[0] * delta[j, t, rows]
                        for f in range(1, 6):
                            w = w + coefficient[f] * delta[j, 2 * f + t, rows]
                        pair.append(w)
                    w = jnp.concatenate(pair, axis=0)
                    high = w.astype(BF16)
                    place = (pl.ds(nu * s + 16 * m, 16), pl.ds(128 * t, 128))
                    wh[place] = high
                    wl[place] = (w - high.astype(F32)).astype(BF16)
        coupling = c_ref[0, c]
        high = coupling.astype(BF16)
        low = (coupling - high.astype(F32)).astype(BF16)
        both = jnp.dot(jnp.concatenate([high, low], axis=0), wh[...], preferred_element_type=F32)
        return total + (both[:nu] + both[nu:]) + jnp.dot(high, wl[...], preferred_element_type=F32)

    total = lax.fori_loop(0, 4, chunk, jnp.zeros((nu, 256), F32))
    out_ref[0, 0] = total[:, :128]
    out_ref[0, 1] = total[:, 128:]


def slots_call(sb, ei, coupling, got, xm, xp, nu):
    blocks = coupling.shape[0]
    vmem = pl.BlockSpec(memory_space=pltpu.VMEM)
    return pl.pallas_call(
        functools.partial(slots_kernel, nu),
        out_shape=jax.ShapeDtypeStruct((blocks, 2, nu, 128), F32),
        grid_spec=pltpu.PrefetchScalarGridSpec(
            num_scalar_prefetch=2,
            grid=(blocks,),
            in_specs=[pl.BlockSpec((1, 4, nu, 256), lambda b, *_: (b, 0, 0, 0)), vmem, vmem, vmem],
            out_specs=pl.BlockSpec((1, 2, nu, 128), lambda b, *_: (b, 0, 0, 0)),
            scratch_shapes=[
                pltpu.VMEM((16, 12, nu, 128), F32),
                pltpu.VMEM((12, 136, 128), F32),
                pltpu.VMEM((256, 256), BF16),
                pltpu.VMEM((256, 256), BF16),
            ],
        ),
        compiler_params=pltpu.CompilerParams(vmem_limit_bytes=40 << 20),
        name="slots",
    )(sb, ei, coupling, got, xm, xp)


def pieces_of(stacked):
    rows = stacked.shape[0]
    split = stacked.reshape(rows, 2, 2, 8, 16, 8).transpose(4, 1, 0, 2, 3, 5)
    center = split.reshape(16, 2, rows, 128)
    above = jnp.pad(center[1:], ((0, 1), (0, 0), (0, 0), (0, 0)))
    below = jnp.pad(center[:-1], ((1, 0), (0, 0), (0, 0), (0, 0)))
    zz = lanes((16, rows, 128)) % 8
    halo = jnp.where(zz == 7, xroll(above[:, 0], 7), 0.0)
    halo = jnp.where(zz == 6, xroll(above[:, 1], 6), halo)
    halo = jnp.where(zz == 0, xroll(below[:, 0], 121), halo)
    halo = jnp.where(zz == 1, xroll(below[:, 1], 122), halo)
    return jnp.concatenate([center, halo[:, None]], axis=1)


def on_device(solution_modes, coefficient_modes, coupling, source_block, expansion_index):
    nu, na = solution_modes.shape[0], coefficient_modes.shape[0]
    stacked = jnp.concatenate([solution_modes, coefficient_modes], axis=0)
    pieces = pieces_of(stacked)
    got = lax.all_to_all(pieces, "modes", 0, 0, tiled=True)
    tiles = lax.axis_size("tiles")
    up = [(i, i + 1) for i in range(tiles - 1)]
    xm = lax.ppermute(got[:, 1], "tiles", up)
    xp = lax.ppermute(got[:, 0], "tiles", [(j, i) for i, j in up])
    packed = coupling[0].reshape(4, 8, nu, nu).transpose(0, 2, 1, 3).reshape(4, nu, 8 * nu)
    packed = lax.all_gather(packed, "modes", axis=0)
    sb = lax.all_gather(source_block[0], "modes", axis=0).reshape(-1)
    ei = lax.all_gather(expansion_index[0], "modes", axis=0).reshape(-1)
    out = slots_call(sb, ei, packed, got, xm, xp, nu)
    back = lax.all_to_all(out, "modes", 0, 0, tiled=True)
    back = back.reshape(16, 2, nu, 2, 8, 8).transpose(2, 1, 3, 4, 0, 5)
    return back.reshape(solution_modes.shape)


def solution(mesh):
    placed = (
        P("modes", "tiles", None, None),
        P("modes", "tiles", None, None),
        P("modes", None, None, None),
        P("modes", None),
        P("modes", None),
    )
    return jax.shard_map(
        on_device,
        mesh=mesh,
        in_specs=placed,
        out_specs=P("modes", "tiles", None, None),
        check_vma=False,
    )
```

time: 237 us -> 150 us (0.63)
  Pallas kernels: 90.9 us -> 23.1 us
  other arithmetic: 20.6 us -> 4.14 us
  blocking collectives: 56.9 us -> 68.8 us
  starting transfers between devices: 15.6 us -> 8.9 us
  waiting for transfers between devices: 4.75 us -> 0.04 us
    pallas_call x1, Pallas kernels: 90.9 us -> 23.1 us  [slots_call(): pl.pallas_call(functools.partial(slots_kernel, nu), out_shape=jax.ShapeDt...]
    all_to_all x0 -> x1, blocking collectives: none -> 21.2 us  [on_device(): got = lax.all_to_all(pieces, 'modes', 0, 0, tiled=True)]
    concatenate x4 -> x0, other arithmetic: 7.19 us -> none  [the longest x1 5.16 us: on_device(): cext = jnp.concatenate([ch, ch, cl], axis=-1)]
    all_gather x1, blocking collectives: 25.5 us -> 18.8 us  [on_device(): sb = lax.all_gather(source_block[0], 'modes', axis=0).reshape(-1)]
    all_to_all x1 -> x0, starting transfers between devices: 6.51 us -> none  [on_device(): got = lax.all_to_all(pieces, 'modes', 0, 0, tiled=True)]
    convert_element_type x2 -> x0, other arithmetic: 5.96 us -> none  [high_low(): return (high.astype(BF16), (value - high).astype(BF16))]
    ppermute x1, waiting for transfers between devices: 4.05 us -> 0.01 us  [on_device(): xp = lax.ppermute(got[:, 0], 'tiles', [(j, i) for i, j in up])]
    slice x36 -> x0, local copies, waits for them, and re-layouts: 2.92 us -> none  [xroll(): return jnp.roll(value, shift, axis=-1)]
  transfers between devices with their start and end apart: 4 -> 3, of which waited for: 1 -> 0; matrix products, arithmetic and copies ran while one was open for 5% -> 17% of each run, Pallas kernels for 0% -> 0%
where the time goes in v2:
time: 150 us; the launch traced here: 149 us
  blocking collectives  68.8 us (46%)
  local copies, waits for them, and re-layouts  30.2 us (20%)
  Pallas kernels  23.1 us (15%)
  between operations  13.6 us (9%)
  starting transfers between devices  8.9 us (6%)
  other arithmetic  4.14 us (3%)
    pallas_call x1, Pallas kernels, slots_call(): pl.pallas_call(functools.partial(slots_kernel, nu), out_shape=jax.ShapeDt...  23.1 us
    all_to_all x1, blocking collectives, on_device(): got = lax.all_to_all(pieces, 'modes', 0, 0, tiled=True)  21.2 us
    all_gather x1, blocking collectives, on_device(): sb = lax.all_gather(source_block[0], 'modes', axis=0).reshape(-1)  18.8 us
    all_gather x1, blocking collectives, on_device(): ei = lax.all_gather(expansion_index[0], 'modes', axis=0).reshape(-1)  16.3 us
    all_to_all x1, blocking collectives, on_device(): back = lax.all_to_all(out, 'modes', 0, 0, tiled=True)  12.6 us
    concatenate x16, local copies, waits for them, and re-layouts, xroll(): return jnp.roll(value, shift, axis=-1)  10.7 us
    ppermute x1, starting transfers between devices, on_device(): xm = lax.ppermute(got[:, 1], 'tiles', up)  6.44 us
    reshape x1, local copies, waits for them, and re-layouts, pieces_of(): center = split.reshape(16, 2, rows, 128)  3.2 us
  transfers between devices with their start and end apart: 3, of which 0 were waited for; matrix products, arithmetic and copies ran while one was open for 17% of the time, Pallas kernels for 0%

profile of v2, /device:TPU:7, one launch (start us, length us, event | category | flops | bytes accessed | tf_op | source)
XLA Modules:
  0.0 148.7 jit_solution(5991213983859945905)
XLA Ops:
  6.5 0.0 copy-start.4
  6.5 0.0 all-gather.4.cloned.1.call-start
  6.5 1.4 copy.62
  7.9 0.8 all_gather_reshape.3
  8.8 0.0 all-gather.4.cloned.1.call-update
  8.8 0.0 copy-done.4
  8.8 1.0 pad_maximum_fusion.1
  9.8 0.6 copy.41
  10.4 1.6 %copy.42 = f32[16,2,40,2,8,8]{2,5,4,3,1,0:T(8,128)} copy(f32[16,2,40,2,8,8]{2,5,0,4,3,1:T(8,128)S(1)} %bitcast.50) | data formatting | bytes 1310720 | tf_op jit(solution)/shard_map/transpose | solution.py:131
  12.0 2.2 %fusion.4 = (f32[15,2,40,2,8,8]{2,5,0,4,3,1:T(8,128)}, f32[15,2,40,2,8,8]{2,5,0,4,3,1:T(8,128)}) fusion(f32[16,2,40,2,8,8]{2,5,0,4,3,1:T(8,128)S(1)} %bitcast.51), kind=kLoop, calls=%fused_computation.32 | loop fusion | bytes 2457600 | tf_op jit(solution)/shard_map/slice | solution.py:133
  14.2 0.0 copy-start.2
  14.2 3.2 %copy.53 = f32[16,2,40,128]{3,2,1,0:T(8,128)} copy(f32[16,2,40,128]{2,3,1,0:T(8,128)} %bitcast.54) | data formatting | bytes 1310720 | tf_op jit(solution)/shard_map/reshape | solution.py:132
  17.4 0.0 copy-done.2
  17.4 0.2 copy.48
  17.7 1.2 fusion.3
  18.9 0.1 slice_bitcast_fusion
  19.0 1.1 copy.52
  20.1 0.0 copy-start.1
  20.1 2.6 %slice_bitcast_fusion.1 = f32[16,1,40,122]{2,3,0,1:T(8,128)} fusion(f32[16,40,128]{1,2,0:T(8,128)} %get-tuple-element.8), kind=kLoop, calls=%fused_computation.9 | loop fusion | bytes 624640 | tf_op jit(solution)/shard_map/jit(_roll_static)/concatenate | solution.py:45
  22.6 2.3 %copy.50 = f32[16,1,40,122]{3,2,1,0:T(8,128)} copy(f32[16,1,40,122]{2,3,0,1:T(8,128)} %slice_bitcast_fusion.1) | data formatting | bytes 624640 | tf_op jit(solution)/shard_map/jit(_roll_static)/concatenate | solution.py:45
  24.9 0.8 slice_bitcast_fusion.7
  25.8 0.2 copy.49
  26.0 0.9 copy.51
  26.9 0.0 copy-done.1
  26.9 0.2 copy.43
  27.2 0.3 fusion.1
  27.5 0.1 slice_bitcast_fusion.2
  27.6 1.1 copy.46
  28.6 0.1 slice_bitcast_fusion.3
  28.7 1.1 copy.44
  29.8 0.0 copy-start.3
  29.8 0.2 copy.45
  30.0 0.2 copy.47
  30.2 1.8 %maximum_select_fusion = f32[16,1,40,128]{3,2,1,0:T(8,128)S(1)} fusion(f32[16,1,40,6]{3,2,1,0:T(8,128)S(1)} %copy.45, f32[16,1,40,122]{3,2,1,0:T(8,128)} %copy.44, f32[16,1,40,7]{3,2,1,0:T(8,128)S(1)} %copy.47, f32[16,1,40,121]{3,2,1,0:T(8,128)} %copy.46, f32[16,1,40,122]{3,2,1,0:T(8,128)} %copy.50, f32[16,1,40,6]{3,2,1,0:T(8,128)S(1)} %copy.49, ...), kind=kLoop, calls=%fused_computation.21 | loop fusion | flops 1064960 | bytes 1639552 | tf_op jit(solution)/shard_map/jit(_where)/select_n | solution.py:139
  32.0 0.0 copy-done.3
  32.0 0.1 pad_maximum_fusion
  32.1 0.0 copy-start.5
  32.1 0.0 copy-start.6
  32.1 21.2 %all_to_all.10.got_ref = f32[16,3,40,128]{3,2,1,0:T(8,128)S(1)} all-to-all(f32[16,3,40,128]{3,2,1,0:T(8,128)S(1)} %pad_maximum_fusion), channel_id=1, replica_groups=mesh['modes'=16,'tiles'=8] {'modes'}, dimensions={0} | all-to-all | bytes 1966080 | tf_op jit(solution)/shard_map/all_to_all | solution.py:147
  53.4 2.5 %collective-permute-start.1 = (f32[16,40,128]{2,1,0:T(8,128)S(1)}, f32[16,40,128]{2,1,0:T(8,128)S(1)}, u32[]{:S(2)}, u32[]{:S(2)}) collective-permute-start(f32[16,40,128]{2,1,0:T(8,128)S(1)} %get-tuple-element.11), channel_id=1, source_target_pairs={{1,0},{2,1},{3,2},{4,3},{5,4},{6,5},{7,6},{9,8},{10,9},{11,10},{12... | collective-permute-start | bytes 983048 | tf_op jit(solution)/shard_map/ppermute | solution.py:151
  55.8 6.4 %collective-permute-start = (f32[16,40,128]{2,1,0:T(8,128)S(1)}, f32[16,40,128]{2,1,0:T(8,128)S(1)}, u32[]{:S(2)}, u32[]{:S(2)}) collective-permute-start(f32[16,40,128]{2,1,0:T(8,128)S(1)} %get-tuple-element.12), channel_id=1, source_target_pairs={{0,1},{1,2},{2,3},{3,4},{4,5},{5,6},{6,7},{8,9},{9,10},{10,11},{11... | collective-permute-start | bytes 983048 | tf_op jit(solution)/shard_map/ppermute | solution.py:150
  62.3 0.0 copy-done.5
  62.3 18.8 %all-gather = s32[16,1,32]{2,1,0:T(1,128)S(1)} all-gather(s32[1,1,32]{2,1,0:T(1,128)S(1)} %bitcast.59), channel_id=1, replica_groups=mesh['modes'=16,'tiles'=8] {'modes'}, dimensions={0}, use_global_device_ids=true | all-gather | bytes 2176 | tf_op jit(solution)/shard_map/all_gather | solution.py:154
  81.1 0.5 broadcast.81
  81.6 0.7 reduce.6
  82.2 0.1 reshape.151.sb_ref
  82.3 0.0 copy-done.6
  82.3 16.3 %all-gather.1 = s32[16,1,32]{2,1,0:T(1,128)S(1)} all-gather(s32[1,1,32]{2,1,0:T(1,128)S(1)} %bitcast.60), channel_id=1, replica_groups=mesh['modes'=16,'tiles'=8] {'modes'}, dimensions={0}, use_global_device_ids=true | all-gather | bytes 2176 | tf_op jit(solution)/shard_map/all_gather | solution.py:155
  98.6 0.7 reduce.7
  99.3 0.1 reshape.152.ei_ref
  99.3 0.0 collective-permute-done.1.xp_ref
  99.3 0.0 collective-permute-done.xm_ref
  99.3 0.0 all-gather.4.cloned.1.call-done.c_ref
  99.4 0.0 copy-start
  99.4 1.6 %copy-done = f32[16,4,32,256]{3,2,1,0:T(8,128)S(1)} copy-done((f32[16,4,32,256]{3,2,1,0:T(8,128)S(1)}, f32[16,4,32,256]{3,2,1,0:T(8,128)}, u32[]{:S(2)}) %copy-start) | copy-done | bytes 2097176
  101.0 23.1 %slots.1 = f32[16,2,32,128]{3,2,1,0:T(8,128)S(1)} custom-call(s32[512]{0:T(512)S(1)} %reshape.151.sb_ref, s32[512]{0:T(512)S(1)} %reshape.152.ei_ref, f32[16,4,32,256]{3,2,1,0:T(8,128)S(1)} %copy-done, f32[16,3,40,128]{3,2,1,0:T(8,128)S(1)} %all_to_all.10.got_ref, f32[16,40,128]{2,1,0:T(8,128)S(1)} %collective-permute-done.xm_ref, ...), custom_call_target="tpu_custom_call" | custom-call | tf_op jit(solution)/shard_map/slots/pallas_call | solution.py:109
  124.1 12.6 %all_to_all.11 = f32[16,2,32,128]{3,2,1,0:T(8,128)S(1)} all-to-all(f32[16,2,32,128]{3,2,1,0:T(8,128)S(1)} %slots.1), channel_id=1, replica_groups=mesh['modes'=16,'tiles'=8] {'modes'}, dimensions={0} | all-to-all | bytes 1048576 | tf_op jit(solution)/shard_map/all_to_all | solution.py:157
  136.6 0.6 copy.56
  137.2 1.6 %copy.57 = f32[32,2,2,8,16,8]{0,5,4,3,2,1:T(8,128)} copy(f32[32,2,2,8,16,8]{0,5,3,2,1,4:T(8,128)S(1)} %bitcast.52) | data formatting | bytes 1048576 | tf_op jit(solution)/shard_map/transpose | solution.py:158
  138.8 3.0 %copy.58 = f32[32,4,8,128]{3,2,1,0:T(8,128)} copy(f32[32,4,8,128]{0,3,2,1:T(8,128)} %bitcast.53) | data formatting | bytes 1048576 | tf_op jit(solution)/shard_map/reshape | solution.py:159
  (6 shorter events, 0.1 us)
Async XLA Ops:
  6.5 2.3 %copy-start.4 = (f32[32,4,8,128]{3,2,1,0:T(8,128)S(1)}, f32[32,4,8,128]{3,2,1,0:T(8,128)}, u32[]{:S(2)}) copy-start(f32[32,4,8,128]{3,2,1,0:T(8,128)} %param.5) | copy-start | bytes 1572868
  6.5 92.8 %all-gather.4.cloned.1.call-start = ((), (), s32[]{:S(2)}) async-start(), calls=%async_computation.2 | async-start | bytes 2228224 | tf_op jit(solution)/shard_map/all_gather | solution.py:153
  14.2 3.2 %copy-start.2 = (f32[15,2,40,2,8,8]{2,5,0,4,3,1:T(8,128)S(1)}, f32[15,2,40,2,8,8]{2,5,0,4,3,1:T(8,128)}, u32[]{:S(2)}) copy-start(f32[15,2,40,2,8,8]{2,5,0,4,3,1:T(8,128)} %get-tuple-element.5) | copy-start | bytes 1843204
  20.1 6.8 %copy-start.1 = (f32[15,2,40,2,8,8]{2,5,0,4,3,1:T(8,128)S(1)}, f32[15,2,40,2,8,8]{2,5,0,4,3,1:T(8,128)}, u32[]{:S(2)}) copy-start(f32[15,2,40,2,8,8]{2,5,0,4,3,1:T(8,128)} %get-tuple-element.6) | copy-start | bytes 1843204
  29.8 2.2 %copy-start.3 = (f32[16,2,40,128]{3,2,1,0:T(8,128)S(1)}, f32[16,2,40,128]{3,2,1,0:T(8,128)}, u32[]{:S(2)}) copy-start(f32[16,2,40,128]{3,2,1,0:T(8,128)} %copy.53) | copy-start | bytes 1966084
  32.1 30.2 %copy-start.5 = (s32[1,32]{1,0:T(1,128)S(1)}, s32[1,32]{1,0:T(1,128)}, u32[]{:S(2)}) copy-start(s32[1,32]{1,0:T(1,128)} %param.8) | copy-start | bytes 388
  32.1 50.2 %copy-start.6 = (s32[1,32]{1,0:T(1,128)S(1)}, s32[1,32]{1,0:T(1,128)}, u32[]{:S(2)}) copy-start(s32[1,32]{1,0:T(1,128)} %param.9) | copy-start | bytes 388
  53.4 46.0 %collective-permute-start.1 = (f32[16,40,128]{2,1,0:T(8,128)S(1)}, f32[16,40,128]{2,1,0:T(8,128)S(1)}, u32[]{:S(2)}, u32[]{:S(2)}) collective-permute-start(f32[16,40,128]{2,1,0:T(8,128)S(1)} %get-tuple-element.11), channel_id=1, source_target_pairs={{1,0},{2,1},{3,2},{4,3},{5,4},{6,5},{7,6},{9,8},{10,9},{11,10},{12... | collective-permute-start | bytes 983048 | tf_op jit(solution)/shard_map/ppermute | solution.py:151
  55.8 43.5 %collective-permute-start = (f32[16,40,128]{2,1,0:T(8,128)S(1)}, f32[16,40,128]{2,1,0:T(8,128)S(1)}, u32[]{:S(2)}, u32[]{:S(2)}) collective-permute-start(f32[16,40,128]{2,1,0:T(8,128)S(1)} %get-tuple-element.12), channel_id=1, source_target_pairs={{0,1},{1,2},{2,3},{3,4},{4,5},{5,6},{6,7},{8,9},{9,10},{10,11},{11... | collective-permute-start | bytes 983048 | tf_op jit(solution)/shard_map/ppermute | solution.py:150
  99.4 1.6 %copy-start = (f32[16,4,32,256]{3,2,1,0:T(8,128)S(1)}, f32[16,4,32,256]{3,2,1,0:T(8,128)}, u32[]{:S(2)}) copy-start(f32[16,4,32,256]{3,2,1,0:T(8,128)} %all-gather.4.cloned.1.call-done.c_ref) | copy-start | bytes 6291460
Sparse Core Ops, SparseCore 0:
  9.0 40.2 all-gather.3

commit v3 on v2

--- a/solution.py
+++ b/solution.py
@@ -39,10 +39,6 @@
 
 def mean(own, other):
     return 0.5 * (own + other)
-
-
-def xroll(value, shift):
-    return jnp.roll(value, shift, axis=-1)
 
 
 def kroll(value, shift):
@@ -92,7 +88,7 @@
                     place = (pl.ds(nu * s + 16 * m, 16), pl.ds(128 * t, 128))
                     wh[place] = high
                     wl[place] = (w - high.astype(F32)).astype(BF16)
-        coupling = c_ref[0, c]
+        coupling = c_ref[0, pl.ds(pl.multiple_of(nu * c, nu), nu)]
         high = coupling.astype(BF16)
         low = (coupling - high.astype(F32)).astype(BF16)
         both = jnp.dot(jnp.concatenate([high, low], axis=0), wh[...], preferred_element_type=F32)
@@ -112,7 +108,7 @@
         grid_spec=pltpu.PrefetchScalarGridSpec(
             num_scalar_prefetch=2,
             grid=(blocks,),
-            in_specs=[pl.BlockSpec((1, 4, nu, 256), lambda b, *_: (b, 0, 0, 0)), vmem, vmem, vmem],
+            in_specs=[pl.BlockSpec((1, 4 * nu + 8, 256), lambda b, *_: (b, 0, 0)), vmem, vmem, vmem],
             out_specs=pl.BlockSpec((1, 2, nu, 128), lambda b, *_: (b, 0, 0, 0)),
             scratch_shapes=[
                 pltpu.VMEM((16, 12, nu, 128), F32),
@@ -126,37 +122,263 @@
     )(sb, ei, coupling, got, xm, xp)
 
 
-def pieces_of(stacked):
-    rows = stacked.shape[0]
-    split = stacked.reshape(rows, 2, 2, 8, 16, 8).transpose(4, 1, 0, 2, 3, 5)
-    center = split.reshape(16, 2, rows, 128)
-    above = jnp.pad(center[1:], ((0, 1), (0, 0), (0, 0), (0, 0)))
-    below = jnp.pad(center[:-1], ((1, 0), (0, 0), (0, 0), (0, 0)))
-    zz = lanes((16, rows, 128)) % 8
-    halo = jnp.where(zz == 7, xroll(above[:, 0], 7), 0.0)
-    halo = jnp.where(zz == 6, xroll(above[:, 1], 6), halo)
-    halo = jnp.where(zz == 0, xroll(below[:, 0], 121), halo)
-    halo = jnp.where(zz == 1, xroll(below[:, 1], 122), halo)
-    return jnp.concatenate([center, halo[:, None]], axis=1)
+def transpose_blocks(rows):
+    lane = lanes(rows[0].shape)
+    for d in (1, 2, 4, 8):
+        keep = (lane // 8) & d == 0
+        fresh = list(rows)
+        for i in range(16):
+            if not i & d:
+                fresh[i] = jnp.where(keep, rows[i], kroll(rows[i + d], 8 * d))
+                fresh[i + d] = jnp.where(keep, kroll(rows[i], 128 - 8 * d), rows[i + d])
+        rows = fresh
+    return rows
+
+
+def cut(value_ref, pieces, count, first):
+    def one(m, carry):
+        place = pl.ds(pl.multiple_of(first + 8 * m, 8), 8)
+        for t in range(2):
+            rows = [value_ref[pl.ds(256 * m + 16 * t + i, 8, stride=32), :] for i in range(16)]
+            for p, value in enumerate(transpose_blocks(rows)):
+                pieces[p + 1, t, place] = value
+        return carry
+
+    lax.fori_loop(0, count // 8, one, 0)
+
+
+def rims(pieces):
+    rows = pieces.shape[2]
+    for t in range(2):
+        pieces[0, t] = jnp.zeros((rows, 128), F32)
+        pieces[17, t] = jnp.zeros((rows, 128), F32)
+
+    def one(p, carry):
+        for m in range(rows // 8):
+            place = pl.ds(8 * m, 8)
+            zz = lanes((8, 128)) % 8
+            rim = jnp.where(zz == 7, kroll(pieces[p + 2, 0, place], 7), 0.0)
+            rim = jnp.where(zz == 6, kroll(pieces[p + 2, 1, place], 6), rim)
+            rim = jnp.where(zz == 0, kroll(pieces[p, 0, place], 121), rim)
+            rim = jnp.where(zz == 1, kroll(pieces[p, 1, place], 122), rim)
+            pieces[p + 1, 2, place] = rim
+        return carry
+
+    lax.fori_loop(0, 16, one, 0)
+
+
+def pack(c_ref, index_ref, held, me):
+    n = c_ref.shape[1]
+    for q in range(4):
+        for h in range(2):
+            for m in range(n // 8):
+                parts = [c_ref[8 * q + 4 * h + l, pl.ds(8 * m, 8), :] for l in range(4)]
+                held[me, pl.ds(n * q + 8 * m, 8), pl.ds(128 * h, 128)] = jnp.concatenate(parts, axis=1)
+    held[me, pl.ds(4 * n, 8), :] = index_ref[...]
+
+
+def remote(src, dst, send, recv, **where):
+    return pltpu.make_async_remote_copy(
+        src_ref=src, dst_ref=dst, send_sem=send, recv_sem=recv,
+        device_id=where, device_id_type=pl.DeviceIdType.MESH)
+
+
+def greet(others):
+    barrier = pltpu.get_barrier_semaphore()
+    for where in others:
+        pl.semaphore_signal(barrier, inc=1, device_id=where, device_id_type=pl.DeviceIdType.MESH)
+    return barrier
+
+
+def spread_kernel(u_ref, a_ref, c_ref, index_ref, got, xm, xp, held, pieces,
+                  p_send, p_recv, m_send, m_recv, q_send, q_recv, c_send, c_recv, own_sem):
+    me, tile = lax.axis_index("modes"), lax.axis_index("tiles")
+    tiles = lax.axis_size("tiles")
+    has_up, has_down = tile < tiles - 1, tile > 0
+    peers = [lax.rem(me + d, 16) for d in range(1, 16)]
+    z, y, core = me // 8, lax.rem(me // 2, 4), lax.rem(me, 2)
+
+    def block(dz, dy, dc):
+        return lax.rem(z + dz, 2) * 8 + lax.rem(y + dy, 4) * 2 + lax.rem(core + dc, 2)
+
+    across = {"modes": block(1, 0, 0), "tiles": lax.rem(tile + tiles // 2, tiles)}
+    barrier = greet([{"modes": p} for p in peers] + [across])
+
+    @pl.when(has_up)
+    def _():
+        pl.semaphore_signal(barrier, inc=1, device_id={"tiles": tile + 1}, device_id_type=pl.DeviceIdType.MESH)
+
+    @pl.when(has_down)
+    def _():
+        pl.semaphore_signal(barrier, inc=1, device_id={"tiles": tile - 1}, device_id_type=pl.DeviceIdType.MESH)
+
+    nu, na = u_ref.shape[0] // 32, a_ref.shape[0] // 32
+    cut(u_ref, pieces, nu, 0)
+    cut(a_ref, pieces, na, nu)
+    rims(pieces)
+    pack(c_ref, index_ref, held, me)
+    zero = jnp.zeros(xm.shape[1:], F32)
+
+    @pl.when(jnp.logical_not(has_down))
+    def _():
+        for j in range(16):
+            xm[j] = zero
+
+    @pl.when(jnp.logical_not(has_up))
+    def _():
+        for j in range(16):
+            xp[j] = zero
+
+    pl.semaphore_wait(barrier, 16 + has_up.astype(jnp.int32) + has_down.astype(jnp.int32))
+    own = pltpu.make_async_copy(pieces.at[me + 1], got.at[me], own_sem)
+    own.start()
+    out = [remote(pieces.at[p + 1], got.at[me], p_send.at[i], p_recv.at[me], modes=p) for i, p in enumerate(peers)]
+    for copy in out:
+        copy.start()
+
+    def share(i, which, **where):
+        copy = remote(held.at[which], held.at[which], c_send.at[i], c_recv.at[which], **where)
+        copy.start()
+        return copy
+
+    def landed(which):
+        remote(held.at[which], held.at[which], c_send.at[0], c_recv.at[which], modes=block(0, 0, 1)).wait_recv()
+
+    sent = [share(i, me, modes=block(0, dy, 0)) for i, dy in enumerate((1, 3, 2))]
+    sent.append(share(3, me, modes=block(1, 0, 0)))
+    sent.append(share(4, me, modes=block(0, 0, 1)))
+
+    def upward(j):
+        return remote(got.at[j, 1], xm.at[j], m_send.at[j], m_recv.at[j], tiles=tile + 1)
+
+    def downward(j):
+        return remote(got.at[j, 0], xp.at[j], q_send.at[j], q_recv.at[j], tiles=tile - 1)
+
+    def forward(j):
+        @pl.when(has_up)
+        def _():
+            upward(j).start()
+
+        @pl.when(has_down)
+        def _():
+            downward(j).start()
+
+    own.wait()
+    forward(me)
+    for d in range(1, 16):
+        source = lax.rem(me + 16 - d, 16)
+        remote(pieces.at[1], got.at[source], p_send.at[0], p_recv.at[source], modes=peers[0]).wait_recv()
+        forward(source)
+
+    for i, dy in enumerate((1, 3, 2)):
+        which = block(0, dy, 0)
+        landed(which)
+        sent.append(share(5 + 2 * i, which, modes=block(0, 0, 1)))
+        where = {"modes": block(1, 0, 0)} if dy == 1 else across
+        sent.append(share(6 + 2 * i, which, **where))
+    for dy in range(4):
+        which = block(1, dy, 0)
+        landed(which)
+        sent.append(share(11 + dy, which, modes=block(0, 0, 1)))
+    for dz in range(2):
+        for dy in range(4):
+            landed(block(dz, dy, 1))
+    for copy in sent + out:
+        copy.wait_send()
+
+    def finish(j, carry):
+        @pl.when(has_up)
+        def _():
+            upward(j).wait_send()
+            remote(got.at[j, 0], xp.at[j], q_send.at[j], q_recv.at[j], tiles=tile + 1).wait_recv()
+
+        @pl.when(has_down)
+        def _():
+            downward(j).wait_send()
+            remote(got.at[j, 1], xm.at[j], m_send.at[j], m_recv.at[j], tiles=tile - 1).wait_recv()
+
+        return carry
+
+    lax.fori_loop(0, 16, finish, 0)
+
+
+def spread(u, a, coupling, index):
+    rows = (u.shape[0] + a.shape[0]) // 32
+    n = coupling.shape[1]
+    vmem = pl.BlockSpec(memory_space=pltpu.VMEM)
+    dma = pltpu.SemaphoreType.DMA
+    return pl.pallas_call(
+        spread_kernel,
+        out_shape=(
+            jax.ShapeDtypeStruct((16, 3, rows, 128), F32),
+            jax.ShapeDtypeStruct((16, rows, 128), F32),
+            jax.ShapeDtypeStruct((16, rows, 128), F32),
+            jax.ShapeDtypeStruct((16, 4 * n + 8, 256), F32),
+        ),
+        in_specs=[vmem] * 4,
+        out_specs=(vmem,) * 4,
+        scratch_shapes=[
+            pltpu.VMEM((18, 3, rows, 128), F32),
+            dma((15,)), dma((16,)), dma((16,)), dma((16,)), dma((16,)), dma((16,)), dma((15,)), dma((16,)), dma,
+        ],
+        compiler_params=pltpu.CompilerParams(collective_id=0, has_side_effects=True, vmem_limit_bytes=40 << 20),
+        name="spread",
+    )(u, a, coupling, index)
+
+
+def gather_kernel(part_ref, out_ref, back, send, recv, own_sem):
+    me = lax.axis_index("modes")
+    peers = [lax.rem(me + d, 16) for d in range(1, 16)]
+    barrier = greet([{"modes": p} for p in peers])
+    pl.semaphore_wait(barrier, 15)
+    own = pltpu.make_async_copy(part_ref.at[me], back.at[me], own_sem)
+    own.start()
+    out = [remote(part_ref.at[p], back.at[me], send.at[i], recv.at[me], modes=p) for i, p in enumerate(peers)]
+    for copy in out:
+        copy.start()
+    own.wait()
+    for d in range(1, 16):
+        source = lax.rem(me + 16 - d, 16)
+        remote(part_ref.at[0], back.at[source], send.at[0], recv.at[source], modes=peers[0]).wait_recv()
+
+    def one(m, carry):
+        place = pl.ds(pl.multiple_of(8 * m, 8), 8)
+        for t in range(2):
+            rows = [back[p, t, place] for p in range(16)]
+            for i, value in enumerate(transpose_blocks(rows)):
+                out_ref[pl.ds(256 * m + 16 * t + i, 8, stride=32), :] = value
+        return carry
+
+    lax.fori_loop(0, part_ref.shape[2] // 8, one, 0)
+    for copy in out:
+        copy.wait_send()
+
+
+def gather(part):
+    vmem = pl.BlockSpec(memory_space=pltpu.VMEM)
+    dma = pltpu.SemaphoreType.DMA
+    return pl.pallas_call(
+        gather_kernel,
+        out_shape=jax.ShapeDtypeStruct((part.shape[2] * 32, 128), F32),
+        in_specs=[vmem],
+        out_specs=vmem,
+        scratch_shapes=[pltpu.VMEM(part.shape, F32), dma((15,)), dma((16,)), dma],
+        compiler_params=pltpu.CompilerParams(collective_id=1, has_side_effects=True, vmem_limit_bytes=40 << 20),
+        name="gather",
+    )(part)
 
 
 def on_device(solution_modes, coefficient_modes, coupling, source_block, expansion_index):
-    nu, na = solution_modes.shape[0], coefficient_modes.shape[0]
-    stacked = jnp.concatenate([solution_modes, coefficient_modes], axis=0)
-    pieces = pieces_of(stacked)
-    got = lax.all_to_all(pieces, "modes", 0, 0, tiled=True)
-    tiles = lax.axis_size("tiles")
-    up = [(i, i + 1) for i in range(tiles - 1)]
-    xm = lax.ppermute(got[:, 1], "tiles", up)
-    xp = lax.ppermute(got[:, 0], "tiles", [(j, i) for i, j in up])
-    packed = coupling[0].reshape(4, 8, nu, nu).transpose(0, 2, 1, 3).reshape(4, nu, 8 * nu)
-    packed = lax.all_gather(packed, "modes", axis=0)
-    sb = lax.all_gather(source_block[0], "modes", axis=0).reshape(-1)
-    ei = lax.all_gather(expansion_index[0], "modes", axis=0).reshape(-1)
-    out = slots_call(sb, ei, packed, got, xm, xp, nu)
-    back = lax.all_to_all(out, "modes", 0, 0, tiled=True)
-    back = back.reshape(16, 2, nu, 2, 8, 8).transpose(2, 1, 3, 4, 0, 5)
-    return back.reshape(solution_modes.shape)
+    nu = solution_modes.shape[0]
+    slots = source_block.shape[1]
+    index = jnp.concatenate([source_block, expansion_index], axis=1).astype(F32)
+    index = jnp.pad(index, ((0, 7), (0, 256 - 2 * slots)))
+    got, xm, xp, held = spread(
+        solution_modes.reshape(-1, 128), coefficient_modes.reshape(-1, 128), coupling[0], index)
+    index = held[:, 4 * nu, :2 * slots].astype(jnp.int32)
+    sb, ei = index[:, :slots].reshape(-1), index[:, slots:].reshape(-1)
+    out = slots_call(sb, ei, held, got, xm, xp, nu)
+    return gather(out).reshape(solution_modes.shape)
 
 
 def solution(mesh):

time: 150 us -> 82.7 us (0.55)
  blocking collectives: 68.8 us -> 0 us
  Pallas kernels: 23.1 us -> 74.6 us
  local copies, waits for them, and re-layouts: 30.2 us -> 7.01 us
  between operations: 13.6 us -> 0.04 us
  starting transfers between devices: 8.9 us -> 0 us
  other arithmetic: 4.14 us -> 0.75 us
    pallas_call x0 -> x2, Pallas kernels: none -> 51.5 us  [the longest x1 38 us: spread(): pl.pallas_call(spread_kernel, out_shape=(jax.ShapeDtypeStruct((16, 3, row...]
    all_gather x2 -> x0, blocking collectives: 35 us -> none  [the longest x1 18.8 us: on_device(): sb = lax.all_gather(source_block[0], 'modes', axis=0).reshape(-1)]
    all_to_all x2 -> x0, blocking collectives: 33.7 us -> none  [the longest x1 21.2 us: on_device(): got = lax.all_to_all(pieces, 'modes', 0, 0, tiled=True)]
    concatenate x17 -> x0, local copies, waits for them, and re-layouts: 11.3 us -> none  [the longest x16 10.7 us: xroll(): return jnp.roll(value, shift, axis=-1)]
    ppermute x2 -> x0, starting transfers between devices: 8.9 us -> none  [the longest x1 6.44 us: on_device(): xm = lax.ppermute(got[:, 1], 'tiles', up)]
    reshape x4 -> x2, local copies, waits for them, and re-layouts: 6.4 us -> 0.85 us  [on_device(): sb, ei = (index[:, :slots].reshape(-1), index[:, slots:].reshape(-1))]
    unnamed x14 -> x11, local copies, waits for them, and re-layouts: 1.61 us -> 5.47 us
    transpose x2 -> x0, local copies, waits for them, and re-layouts: 3.2 us -> none  [the longest x1 1.6 us: pieces_of(): split = stacked.reshape(rows, 2, 2, 8, 16, 8).transpose(4, 1, 0, 2, 3, 5)]
  transfers between devices with their start and end apart: 3 -> 0, of which waited for: 0 -> 0; matrix products, arithmetic and copies ran while one was open for 17% -> 0% of each run, Pallas kernels for 0% -> 0%
where the time goes in v3:
time: 82.7 us; the launch traced here: 82.4 us
  Pallas kernels  74.6 us (90%)
  local copies, waits for them, and re-layouts  7.01 us (8%)
    pallas_call x1, Pallas kernels, spread(): pl.pallas_call(spread_kernel, out_shape=(jax.ShapeDtypeStruct((16, 3, row...  38 us
    pallas_call x1, Pallas kernels, slots_call(): pl.pallas_call(functools.partial(slots_kernel, nu), out_shape=jax.ShapeDt...  23.1 us
    pallas_call x1, Pallas kernels, gather(): pl.pallas_call(gather_kernel, out_shape=jax.ShapeDtypeStruct((part.shape[...  13.5 us
    unnamed x11, local copies, waits for them, and re-layouts  5.47 us

profile of v3, /device:TPU:7, one launch (start us, length us, event | category | flops | bytes accessed | tf_op | source)
XLA Modules:
  0.0 82.4 jit_solution(5249080465427502504)
XLA Ops:
  0.0 0.7 add_convert_fusion
  0.8 0.0 copy-start
  0.8 1.0 %copy-done = f32[32,4,8,128]{3,2,1,0:T(8,128)S(1)} copy-done((f32[32,4,8,128]{3,2,1,0:T(8,128)S(1)}, f32[32,4,8,128]{3,2,1,0:T(8,128)}, u32[]{:S(2)}) %copy-start) | copy-done | bytes 524312
  1.8 0.0 copy-start.1
  1.8 1.0 %copy-done.1 = f32[1,32,32,32]{3,2,1,0:T(8,128)S(1)} copy-done((f32[1,32,32,32]{3,2,1,0:T(8,128)S(1)}, f32[1,32,32,32]{3,2,1,0:T(8,128)}, u32[]{:S(2)}) %copy-start.1) | copy-done | bytes 131096
  2.8 0.0 copy-start.4
  2.8 0.9 %copy-done.4 = f32[8,4,8,128]{3,2,1,0:T(8,128)S(1)} copy-done((f32[8,4,8,128]{3,2,1,0:T(8,128)S(1)}, f32[8,4,8,128]{3,2,1,0:T(8,128)}, u32[]{:S(2)}) %copy-start.4) | copy-done | bytes 131096
  3.7 38.0 %spread.1 = (f32[16,3,40,128]{3,2,1,0:T(8,128)S(1)}, f32[16,40,128]{2,1,0:T(8,128)S(1)}, f32[16,40,128]{2,1,0:T(8,128)S(1)}, f32[16,136,256]{2,1,0:T(8,128)S(1)}) custom-call(f32[1024,128]{1,0:T(8,128)S(1)} %bitcast.6, f32[256,128]{1,0:T(8,128)S(1)} %bitcast.8, f32[32,32,32]{2,1,0:T(8,128)S(1)} %bitcast.7, f32[8,256]{1,0:T(8,128)S(1)} %pad.4.index_ref), custom_call_target="tpu_custom_call" | custom-call | tf_op jit(solution)/shard_map/spread/pallas_call | solution.py:310
  41.8 0.0 copy-start.2
  41.8 0.7 copy-done.2
  42.5 0.7 fusion
  43.2 0.8 reshape.47.ei_ref
  44.0 0.1 reshape.46.sb_ref
  44.1 0.0 copy-start.3
  44.1 1.0 %copy-done.3 = f32[16,40,128]{2,1,0:T(8,128)S(1)} copy-done((f32[16,40,128]{2,1,0:T(8,128)S(1)}, f32[16,40,128]{2,1,0:T(8,128)}, u32[]{:S(2)}) %copy-start.3) | copy-done | bytes 327704
  45.0 23.1 %slots.1.part_ref = f32[16,2,32,128]{3,2,1,0:T(8,128)S(1)} custom-call(s32[512]{0:T(512)S(1)} %reshape.46.sb_ref, s32[512]{0:T(512)S(1)} %reshape.47.ei_ref, f32[16,136,256]{2,1,0:T(8,128)S(1)} %get-tuple-element.9.c_ref, f32[16,3,40,128]{3,2,1,0:T(8,128)S(1)} %get-tuple-element.10.got_ref, f32[16,40,128]{2,1,0:T(8,128)S(1)} %get-tuple-element.11.xm_ref, ...), custom_call_target="tpu_custom_call" | custom-call | tf_op jit(solution)/shard_map/slots/pallas_call | solution.py:105
  68.2 13.5 %gather.1 = f32[1024,128]{1,0:T(8,128)S(1)} custom-call(f32[16,2,32,128]{3,2,1,0:T(8,128)S(1)} %slots.1.part_ref), custom_call_target="tpu_custom_call" | custom-call | tf_op jit(solution)/shard_map/gather/pallas_call | solution.py:360
  81.6 0.8 copy.7
  (2 shorter events, 0.0 us)
Async XLA Ops:
  0.8 1.0 %copy-start = (f32[32,4,8,128]{3,2,1,0:T(8,128)S(1)}, f32[32,4,8,128]{3,2,1,0:T(8,128)}, u32[]{:S(2)}) copy-start(f32[32,4,8,128]{3,2,1,0:T(8,128)} %param.5) | copy-start | bytes 1572868
  1.8 1.0 %copy-start.1 = (f32[1,32,32,32]{3,2,1,0:T(8,128)S(1)}, f32[1,32,32,32]{3,2,1,0:T(8,128)}, u32[]{:S(2)}) copy-start(f32[1,32,32,32]{3,2,1,0:T(8,128)} %param.7) | copy-start | bytes 393220
  2.8 0.9 %copy-start.4 = (f32[8,4,8,128]{3,2,1,0:T(8,128)S(1)}, f32[8,4,8,128]{3,2,1,0:T(8,128)}, u32[]{:S(2)}) copy-start(f32[8,4,8,128]{3,2,1,0:T(8,128)} %param.6) | copy-start | bytes 393220
  41.8 0.7 copy-start.2
  44.1 1.0 %copy-start.3 = (f32[16,40,128]{2,1,0:T(8,128)S(1)}, f32[16,40,128]{2,1,0:T(8,128)}, u32[]{:S(2)}) copy-start(f32[16,40,128]{2,1,0:T(8,128)} %copy-done.2) | copy-start | bytes 983044

commit v4 on v0

v4 whole, which is shorter than its diff:
```python
import functools

import jax
import jax.numpy as jnp
from jax import lax
from jax.experimental import pallas as pl
from jax.experimental.pallas import tpu as pltpu
from jax.sharding import PartitionSpec as P

F32, BF16 = jnp.float32, jnp.bfloat16


def lanes(shape):
    return lax.broadcasted_iota(jnp.int32, shape, len(shape) - 1)


def difference(own, other):
    return own - other


def mean(own, other):
    return 0.5 * (own + other)


def kroll(value, shift):
    return pltpu.roll(value, shift, value.ndim - 1)


def transpose_blocks(rows):
    lane = lanes(rows[0].shape)
    for d in (1, 2, 4, 8):
        keep = (lane // 8) & d == 0
        fresh = list(rows)
        for i in range(16):
            if not i & d:
                fresh[i] = jnp.where(keep, rows[i], kroll(rows[i + d], 8 * d))
                fresh[i + d] = jnp.where(keep, kroll(rows[i], 128 - 8 * d), rows[i + d])
        rows = fresh
    return rows


def remote(src, dst, send, recv, **where):
    return pltpu.make_async_remote_copy(
        src_ref=src, dst_ref=dst, send_sem=send, recv_sem=recv,
        device_id=where, device_id_type=pl.DeviceIdType.MESH)


def greet(others):
    barrier = pltpu.get_barrier_semaphore()
    for where in others:
        pl.semaphore_signal(barrier, inc=1, device_id=where, device_id_type=pl.DeviceIdType.MESH)
    return barrier


def face_tiles(comb, x0, x1, below, above, r_minus, r_plus):
    lane = lanes(x0.shape)
    zz, yy, low = lane % 8, (lane // 8) % 8, lane < 64
    zero = jnp.zeros_like(x0)
    r0, r1 = kroll(x0, 64), kroll(x1, 64)
    yield comb(x0, jnp.where(low, r0, r1))
    yield comb(x1, jnp.where(low, r1, r_plus))
    yield comb(x0, jnp.where(low, r_minus, r0))
    yield comb(x1, jnp.where(low, r0, r1))
    for x in (x0, x1):
        yield comb(x, jnp.where(yy < 7, kroll(x, 120), zero))
    for x in (x0, x1):
        yield comb(x, jnp.where(yy > 0, kroll(x, 8), zero))
    for x, rim in zip((x0, x1), above):
        yield comb(x, jnp.where(zz < 7, kroll(x, 127), rim))
    for x, rim in zip((x0, x1), below):
        yield comb(x, jnp.where(zz > 0, kroll(x, 1), rim))


def cut(value_ref, pieces, count, first, span):
    def one(m, carry):
        for t in range(2):
            place = pl.ds(pl.multiple_of(span * t + first + 8 * m, 8), 8)
            rows = [value_ref[pl.ds(256 * m + 16 * t + i, 8, stride=32), :] for i in range(16)]
            for p, value in enumerate(transpose_blocks(rows)):
                pieces[p + 1, place] = value
        return carry

    lax.fori_loop(0, count // 8, one, 0)


def rims(pieces, nu, na):
    span = nu + na
    for q in (0, 17):
        pieces[q, pl.ds(0, 2 * span)] = jnp.zeros((2 * span, 128), F32)

    def one(p, carry):
        zz = lanes((8, 128)) % 8

        def rim(first, spots, base):
            for (t, side), spot in spots:
                value = pieces[p + 2 * side, pl.ds(span * t + first, 8)]
                shift = (spot - (0 if side else 7)) % 128
                base = jnp.where(zz == spot, kroll(value, shift), base)
            return base

        outer = (((0, 1), 7), ((1, 1), 6), ((0, 0), 0), ((1, 0), 1))
        inner = (((0, 1), 5), ((1, 1), 4), ((0, 0), 2), ((1, 0), 3))
        for m in range(nu // 16):
            value = rim(8 * m, outer, jnp.zeros((8, 128), F32))
            pieces[p + 1, pl.ds(2 * span + 8 * m, 8)] = rim(nu // 2 + 8 * m, inner, value)
        for m in range(na // 8):
            pieces[p + 1, pl.ds(2 * span + nu // 2 + 8 * m, 8)] = rim(nu + 8 * m, outer, jnp.zeros((8, 128), F32))
        return carry

    lax.fori_loop(0, 16, one, 0, unroll=2)


def pack(c_ref, held, me):
    n = c_ref.shape[1]
    for q in range(4):
        for h in range(2):
            for m in range(n // 8):
                parts = [c_ref[8 * q + 4 * h + l, pl.ds(8 * m, 8), :] for l in range(4)]
                held[me, pl.ds(n * q + 8 * m, 8), pl.ds(128 * h, 128)] = jnp.concatenate(parts, axis=1)


def kernel(u_hbm, a_hbm, c_hbm, sb_ref, ei_ref, out_ref,
           u_ref, a_ref, c_ref, pieces, got, up_out, down_out, from_down, from_up, held, part, back,
           delta, faces, wh, wl, index_v, index_s,
           in_sem, p_send, p_recv, m_send, m_recv, q_send, q_recv, c_send, c_recv, o_send, o_recv, i_send, i_recv, own_sem):
    me, tile = lax.axis_index("modes"), lax.axis_index("tiles")
    tiles = lax.axis_size("tiles")
    has_up, has_down = tile < tiles - 1, tile > 0
    z, y, core = me // 8, lax.rem(me // 2, 4), lax.rem(me, 2)
    nu, na = u_ref.shape[0] // 32, a_ref.shape[0] // 32
    span = nu + na
    slots = c_ref.shape[0]

    def block(dz, dy, dc):
        return lax.rem(z + dz, 2) * 8 + lax.rem(y + dy, 4) * 2 + lax.rem(core + dc, 2)

    loads = [pltpu.make_async_copy(s, d, in_sem.at[i])
             for i, (s, d) in enumerate(((u_hbm, u_ref), (a_hbm, a_ref), (c_hbm, c_ref)))]
    for load in loads:
        load.start()
    opposite = lax.rem(tile + tiles // 2, tiles)
    chips = ((0, 0), (0, 1), (0, 3), (1, 0), (0, 2), (1, 1), (1, 3), (1, 2))
    offsets = [(dz, dy, dc) for dz, dy in chips for dc in range(2)][1:]
    barrier = greet([{"modes": block(*o)} for o in offsets] + [{"modes": block(1, 0, 0), "tiles": opposite}])

    @pl.when(has_up)
    def _():
        pl.semaphore_signal(barrier, inc=1, device_id={"tiles": tile + 1}, device_id_type=pl.DeviceIdType.MESH)

    @pl.when(has_down)
    def _():
        pl.semaphore_signal(barrier, inc=1, device_id={"tiles": tile - 1}, device_id_type=pl.DeviceIdType.MESH)

    loads[0].wait()
    cut(u_ref, pieces, nu, 0, span)
    loads[1].wait()
    cut(a_ref, pieces, na, nu, span)
    rims(pieces, nu, na)
    index_v[me] = jnp.zeros((8, 128), jnp.int32)
    index_v[me, pl.ds(0, 1), pl.ds(0, slots)] = sb_ref[...]
    index_v[me, pl.ds(1, 1), pl.ds(0, slots)] = ei_ref[...]

    @pl.when(jnp.logical_not(has_down))
    def _():
        from_down[...] = jnp.zeros(from_down.shape, F32)

    @pl.when(jnp.logical_not(has_up))
    def _():
        from_up[...] = jnp.zeros(from_up.shape, F32)

    pl.semaphore_wait(barrier, 16 + has_up.astype(jnp.int32) + has_down.astype(jnp.int32))

    own = pltpu.make_async_copy(pieces.at[me + 1], got.at[me], own_sem)
    own.start()
    sends = []
    for i, o in enumerate(offsets):
        copy = remote(pieces.at[block(*o) + 1], got.at[me], p_send.at[i], p_recv.at[me], modes=block(*o))
        copy.start()
        sends.append(copy)
    for i, o in enumerate(offsets):
        copy = remote(index_v.at[me], index_v.at[me], i_send.at[i], i_recv.at[me], modes=block(*o))
        copy.start()
        sends.append(copy)
    loads[2].wait()
    pack(c_ref, held, me)

    def upward(g):
        return remote(up_out.at[g], from_down.at[g], m_send.at[g], m_recv.at[g], tiles=tile + 1)

    def downward(g):
        return remote(down_out.at[g], from_up.at[g], q_send.at[g], q_recv.at[g], tiles=tile - 1)

    low = lanes((8, 128)) < 64
    own.wait()
    for dz, dy in chips:
        for dc in range(2):
            if (dz, dy, dc) != (0, 0, 0):
                source = block(dz, dy, dc)
                remote(pieces.at[1], got.at[source], p_send.at[0], p_recv.at[source], modes=source).wait_recv()
        g = block(dz, dy, 0) // 2
        for m in range(span // 8):
            first = pl.ds(8 * m, 8)
            second = pl.ds(span + 8 * m, 8)
            up_out[g, first] = jnp.where(low, kroll(got[2 * g, second], 64), got[2 * g + 1, second])
            down_out[g, first] = jnp.where(low, got[2 * g, first], kroll(got[2 * g + 1, first], 64))

        @pl.when(has_up)
        def _():
            upward(g).start()

        @pl.when(has_down)
        def _():
            downward(g).start()

    def share(i, which, modes, to):
        return remote(held.at[which], held.at[which], c_send.at[i], c_recv.at[which], modes=modes, tiles=to)

    for i, dy in enumerate((1, 3, 2)):
        share(i, me, block(0, dy, 0), tile).start()
    share(3, me, block(1, 0, 0), tile).start()
    share(4, me, block(0, 0, 1), tile).start()
    for o in offsets:
        source = block(*o)
        remote(index_v.at[source], index_v.at[source], i_send.at[0], i_recv.at[source], modes=source).wait_recv()
    indices = pltpu.make_async_copy(index_v, index_s, own_sem)
    indices.start()

    def prepare(i, carry):
        dz, r = i // 4, i % 4
        g = block(dz, r + (r // 2) * (1 - 2 * (r % 2)), 0) // 2

        @pl.when(has_up)
        def _():
            remote(down_out.at[g], from_up.at[g], q_send.at[g], q_recv.at[g], tiles=tile + 1).wait_recv()

        @pl.when(has_down)
        def _():
            remote(up_out.at[g], from_down.at[g], m_send.at[g], m_recv.at[g], tiles=tile - 1).wait_recv()

        for odd in range(2):
            j = 2 * g + odd

            def tiles_of(first, rim, shifts):
                minus, plus = from_down[g, pl.ds(first, 8)], from_up[g, pl.ds(first, 8)]
                minus, plus = (kroll(minus, 64), plus) if odd else (minus, kroll(plus, 64))
                value = got[j, pl.ds(2 * span + rim, 8)]
                below = [kroll(value, s % 128) if s else value for s in shifts[:2]]
                above = [kroll(value, s % 128) if s else value for s in shifts[2:]]
                return got[j, pl.ds(first, 8)], got[j, pl.ds(span + first, 8)], below, above, minus, plus

            for m in range(nu // 8):
                lower = m < nu // 16
                rim = 8 * m if lower else 8 * m - nu // 2
                parts = tiles_of(8 * m, rim, (0, -1, 0, 1) if lower else (-2, -3, 2, 3))
                for f, value in enumerate(face_tiles(difference, *parts)):
                    delta[j, f, pl.ds(8 * m, 8)] = value
            place = pl.ds(pl.multiple_of(8 * j, 8), 8)
            for f, value in enumerate(face_tiles(mean, *tiles_of(nu, nu // 2, (0, -1, 0, 1)))):
                faces[f, place] = value
        return carry

    lax.fori_loop(0, 8, prepare, 0)
    indices.wait()

    def build(b, c, buffer):
        for s in range(8):
            slot = c * 8 + s
            j = index_s[b, 0, slot]
            k = index_s[b, 1, slot]
            for t in range(2):
                coefficient = [faces[2 * f + t, pl.ds(k, 8, stride=0)] for f in range(6)]
                for m in range(nu // 16):
                    pair = []
                    for h in range(2):
                        rows = pl.ds(16 * m + 8 * h, 8)
                        w = coefficient[0] * delta[j, t, rows]
                        for f in range(1, 6):
                            w = w + coefficient[f] * delta[j, 2 * f + t, rows]
                        pair.append(w)
                    w = jnp.concatenate(pair, axis=0)
                    high = w.astype(BF16)
                    place = (buffer, pl.ds(nu * s + 16 * m, 16), pl.ds(128 * t, 128))
                    wh[place] = high
                    wl[place] = (w - high.astype(F32)).astype(BF16)

    def product(b, c, buffer):
        coupling = held[b, pl.ds(nu * c, nu)]
        high = coupling.astype(BF16)
        small = (coupling - high.astype(F32)).astype(BF16)
        both = jnp.dot(jnp.concatenate([high, small], axis=0), wh[buffer], preferred_element_type=F32)
        return (both[:nu] + both[nu:]) + jnp.dot(high, wl[buffer], preferred_element_type=F32)

    def number(i):
        k = i // 2
        r = k % 4
        return k // 4, r + (r // 2) * (1 - 2 * (r % 2)), i % 2

    def deliver(i):
        b = block(*number(i))
        return remote(part.at[b], back.at[me], o_send.at[i - 1], o_recv.at[me], modes=b)

    def advance(i, carry):
        dz, dy, dc = number(i)
        b = block(dz, dy, dc)

        @pl.when(i > 0)
        def _():
            share(0, b, block(0, 0, 1), tile).wait_recv()

        @pl.when(jnp.logical_and(i > 1, dc == 0))
        def _():
            share(4 + i // 2, b, block(0, 0, 1), tile).start()

        @pl.when(jnp.logical_and(jnp.logical_and(i > 1, dc == 0), dz == 0))
        def _():
            share(11 + i // 2, b, block(1, 0, 0), lax.rem(tile + (dy // 2) * (tiles // 2), tiles)).start()

        total = None
        for c in range(slots // 8):
            build(b, c, c % 2)
            term = product(b, c, c % 2)
            total = term if total is None else total + term

        part[b, 0] = total[:, :128]
        part[b, 1] = total[:, 128:]

        @pl.when(i == 0)
        def _():
            back[me, 0] = total[:, :128]
            back[me, 1] = total[:, 128:]

        @pl.when(i > 1)
        def _():
            deliver(i - 1).start()

        return carry

    lax.fori_loop(0, 16, advance, 0)
    deliver(15).start()

    for dz, dy, dc in offsets:
        source = block(dz, dy, dc)
        remote(part.at[0], back.at[source], o_send.at[0], o_recv.at[source], modes=source).wait_recv()

    def restore(m, carry):
        place = pl.ds(pl.multiple_of(8 * m, 8), 8)
        for t in range(2):
            rows = [back[p, t, place] for p in range(16)]
            for i, value in enumerate(transpose_blocks(rows)):
                out_ref[pl.ds(256 * m + 16 * t + i, 8, stride=32), :] = value
        return carry

    lax.fori_loop(0, nu // 8, restore, 0)
    for copy in sends:
        copy.wait_send()
    for i in range(15):
        share(i, me, block(0, 0, 1), tile).wait_send()
        deliver(i + 1).wait_send()
    for g in range(8):
        @pl.when(has_up)
        def _():
            upward(g).wait_send()

        @pl.when(has_down)
        def _():
            downward(g).wait_send()


def on_device(solution_modes, coefficient_modes, coupling, source_block, expansion_index):
    nu, na = solution_modes.shape[0], coefficient_modes.shape[0]
    span, slots = nu + na, source_block.shape[1]
    rows = 2 * span + nu // 2 + na
    vmem = pl.BlockSpec(memory_space=pltpu.VMEM)
    hbm = pl.BlockSpec(memory_space=pl.ANY)
    dma = pltpu.SemaphoreType.DMA
    out = pl.pallas_call(
        kernel,
        out_shape=jax.ShapeDtypeStruct((nu * 32, 128), F32),
        in_specs=[hbm, hbm, hbm, vmem, vmem],
        out_specs=vmem,
        scratch_shapes=[
            pltpu.VMEM((nu * 32, 128), F32), pltpu.VMEM((na * 32, 128), F32), pltpu.VMEM((slots, nu, nu), F32),
            pltpu.VMEM((18, rows, 128), F32), pltpu.VMEM((16, rows, 128), F32),
            pltpu.VMEM((8, span, 128), F32), pltpu.VMEM((8, span, 128), F32),
            pltpu.VMEM((8, span, 128), F32), pltpu.VMEM((8, span, 128), F32),
            pltpu.VMEM((16, slots // 8 * nu, 256), F32),
            pltpu.VMEM((16, 2, nu, 128), F32), pltpu.VMEM((16, 2, nu, 128), F32),
            pltpu.VMEM((16, 12, nu, 128), F32), pltpu.VMEM((12, 16 * na + 8, 128), F32),
            pltpu.VMEM((2, 8 * nu, 256), BF16), pltpu.VMEM((2, 8 * nu, 256), BF16),
            pltpu.VMEM((16, 8, 128), jnp.int32), pltpu.SMEM((16, 8, 128), jnp.int32),
            dma((3,)), dma((15,)), dma((16,)), dma((8,)), dma((8,)), dma((8,)), dma((8,)),
            dma((15,)), dma((16,)), dma((15,)), dma((16,)), dma((15,)), dma((16,)), dma,
        ],
        compiler_params=pltpu.CompilerParams(collective_id=0, has_side_effects=True, vmem_limit_bytes=56 << 20),
        name="galerkin",
    )(solution_modes.reshape(-1, 128), coefficient_modes.reshape(-1, 128), coupling[0], source_block, expansion_index)
    return out.reshape(solution_modes.shape)


def solution(mesh):
    placed = (
        P("modes", "tiles", None, None),
        P("modes", "tiles", None, None),
        P("modes", None, None, None),
        P("modes", None),
        P("modes", None),
    )
    return jax.shard_map(
        on_device,
        mesh=mesh,
        in_specs=placed,
        out_specs=P("modes", "tiles", None, None),
        check_vma=False,
    )
```

time: 710 us -> 51.7 us (0.07); the launches traced: 699 us -> 51.5 us
  local copies, waits for them, and re-layouts: 177 us -> 1.87 us
  other arithmetic: 161 us -> 0 us
  loops' own time: 138 us -> 0 us
  matrix products: 106 us -> 0 us
  waiting for transfers between devices: 94 us -> 0 us
  Pallas kernels: 0 us -> 49.6 us
  between operations: 13.4 us -> 0.01 us
  starting transfers between devices: 8.9 us -> 0 us
    another operation x1 -> x0, loops' own time: 138 us -> none  [block_output(): lax.scan(advance, start, jnp.arange(source_rows.shape[0], dtype=jnp.int32))]
    dot_general x32 -> x0, matrix products: 106 us -> none  [slot_term(): jnp.einsum('ij,jxyz->ixyz', block_matrix, source_modes, precision=lax.Pre...]
    all_gather x1 -> x0, waiting for transfers between devices: 91.4 us -> none  [on_device(): everyone = lax.all_gather(rimmed, 'modes', axis=0, tiled=True)]
    add x32 -> x0, other arithmetic: 84.6 us -> none  [advance(): return (running + term, None)]
    mul x99 -> x0, other arithmetic: 75.5 us -> none  [the longest x32 42.9 us: divergence(): along_third * (blended[:, 1:-1, 1:-1, :-1] - blended[:, 1:-1, 1:-1, 1:])]
    mul x96 -> x0, local copies, waits for them, and re-layouts: 72.4 us -> none  [the longest x32 24.5 us: divergence(): along_third * (blended[:, 1:-1, 1:-1, :-1] - blended[:, 1:-1, 1:-1, 1:])]
    dynamic_slice x96 -> x0, local copies, waits for them, and re-layouts: 59.4 us -> none  [the longest x32 19.9 us: advance(): expansion = expansion_rows[slot_index]]
    pallas_call x0 -> x1, Pallas kernels: none -> 49.6 us  [on_device(): pl.pallas_call(kernel, out_shape=jax.ShapeDtypeStruct((nu * 32, 128), F32...]
  transfers between devices with their start and end apart: 3 -> 0, of which waited for: 3 -> 0; matrix products, arithmetic and copies ran while one was open for 0% -> 0% of each run, Pallas kernels for 0% -> 0%
where the time goes in v4:
time: 51.7 us; the launch traced here: 51.5 us
  Pallas kernels  49.6 us (96%)
  local copies, waits for them, and re-layouts  1.87 us (4%)
    pallas_call x1, Pallas kernels, on_device(): pl.pallas_call(kernel, out_shape=jax.ShapeDtypeStruct((nu * 32, 128), F32...  49.6 us
    unnamed x1, local copies, waits for them, and re-layouts  1.87 us

profile of v4, /device:TPU:7, one launch (start us, length us, event | category | flops | bytes accessed | tf_op | source)
XLA Modules:
  0.0 51.5 jit_solution(17558935447943251033)
XLA Ops:
  0.0 49.6 %galerkin.1 = f32[1024,128]{1,0:T(8,128)} custom-call(f32[1024,128]{1,0:T(8,128)} %bitcast.5, f32[256,128]{1,0:T(8,128)} %bitcast.7, f32[32,32,32]{2,1,0:T(8,128)} %bitcast.6, s32[1,32]{1,0:T(1,128)} %sb_ref.1, s32[1,32]{1,0:T(1,128)} %ei_ref.1), custom_call_target="tpu_custom_call" | custom-call | tf_op jit(solution)/shard_map/galerkin/pallas_call | solution.py:376
  49.6 1.9 %copy.7 = f32[32,4,8,128]{3,2,1,0:T(8,128)} copy(f32[32,4,8,128]{3,2,1,0:T(8,128)} %bitcast.4) | data formatting | bytes 1048576

commit v5 on v4

--- a/solution.py
+++ b/solution.py
@@ -121,7 +121,7 @@
 
 def kernel(u_hbm, a_hbm, c_hbm, sb_ref, ei_ref, out_ref,
            u_ref, a_ref, c_ref, pieces, got, up_out, down_out, from_down, from_up, held, part, back,
-           delta, faces, wh, wl, index_v, index_s,
+           delta, faces, mixed, index_v, index_s,
            in_sem, p_send, p_recv, m_send, m_recv, q_send, q_recv, c_send, c_recv, o_send, o_recv, i_send, i_recv, own_sem):
     me, tile = lax.axis_index("modes"), lax.axis_index("tiles")
     tiles = lax.axis_size("tiles")
@@ -156,9 +156,9 @@
     loads[1].wait()
     cut(a_ref, pieces, na, nu, span)
     rims(pieces, nu, na)
-    index_v[me] = jnp.zeros((8, 128), jnp.int32)
-    index_v[me, pl.ds(0, 1), pl.ds(0, slots)] = sb_ref[...]
-    index_v[me, pl.ds(1, 1), pl.ds(0, slots)] = ei_ref[...]
+    index_v[me] = jnp.zeros((1, 128), jnp.int32)
+    index_v[me, :, pl.ds(0, slots)] = sb_ref[...]
+    index_v[me, :, pl.ds(slots, slots)] = ei_ref[...]
 
     @pl.when(jnp.logical_not(has_down))
     def _():
@@ -215,10 +215,10 @@
     def share(i, which, modes, to):
         return remote(held.at[which], held.at[which], c_send.at[i], c_recv.at[which], modes=modes, tiles=to)
 
-    for i, dy in enumerate((1, 3, 2)):
-        share(i, me, block(0, dy, 0), tile).start()
-    share(3, me, block(1, 0, 0), tile).start()
-    share(4, me, block(0, 0, 1), tile).start()
+    share(0, me, block(0, 1, 0), tile).start()
+    share(1, me, block(0, 3, 0), tile).start()
+    share(2, me, block(1, 0, 0), tile).start()
+    share(3, me, block(0, 0, 1), tile).start()
     for o in offsets:
         source = block(*o)
         remote(index_v.at[source], index_v.at[source], i_send.at[0], i_recv.at[source], modes=source).wait_recv()
@@ -266,7 +266,7 @@
         for s in range(8):
             slot = c * 8 + s
             j = index_s[b, 0, slot]
-            k = index_s[b, 1, slot]
+            k = index_s[b, 0, slots + slot]
             for t in range(2):
                 coefficient = [faces[2 * f + t, pl.ds(k, 8, stride=0)] for f in range(6)]
                 for m in range(nu // 16):
@@ -277,23 +277,26 @@
                         for f in range(1, 6):
                             w = w + coefficient[f] * delta[j, 2 * f + t, rows]
                         pair.append(w)
-                    w = jnp.concatenate(pair, axis=0)
-                    high = w.astype(BF16)
-                    place = (buffer, pl.ds(nu * s + 16 * m, 16), pl.ds(128 * t, 128))
-                    wh[place] = high
-                    wl[place] = (w - high.astype(F32)).astype(BF16)
+                    for h in range(2):
+                        mixed[buffer, pl.ds(nu * s + 16 * m + 8 * h, 8), pl.ds(128 * t, 128)] = pair[h]
 
     def product(b, c, buffer):
         coupling = held[b, pl.ds(nu * c, nu)]
         high = coupling.astype(BF16)
         small = (coupling - high.astype(F32)).astype(BF16)
-        both = jnp.dot(jnp.concatenate([high, small], axis=0), wh[buffer], preferred_element_type=F32)
-        return (both[:nu] + both[nu:]) + jnp.dot(high, wl[buffer], preferred_element_type=F32)
+        w = mixed[buffer]
+        w_high = w.astype(BF16)
+        w_small = (w - w_high.astype(F32)).astype(BF16)
+        both = jnp.dot(jnp.concatenate([high, small], axis=0), w_high, preferred_element_type=F32)
+        return (both[:nu] + both[nu:]) + jnp.dot(high, w_small, preferred_element_type=F32)
 
     def number(i):
         k = i // 2
-        r = k % 4
+        r = (k % 4 + k // 4) % 4
         return k // 4, r + (r // 2) * (1 - 2 * (r % 2)), i % 2
+
+    def landed(which):
+        share(0, which, block(0, 0, 1), tile).wait_recv()
 
     def deliver(i):
         b = block(*number(i))
@@ -303,23 +306,38 @@
         dz, dy, dc = number(i)
         b = block(dz, dy, dc)
 
-        @pl.when(i > 0)
-        def _():
-            share(0, b, block(0, 0, 1), tile).wait_recv()
-
-        @pl.when(jnp.logical_and(i > 1, dc == 0))
-        def _():
-            share(4 + i // 2, b, block(0, 0, 1), tile).start()
-
-        @pl.when(jnp.logical_and(jnp.logical_and(i > 1, dc == 0), dz == 0))
-        def _():
-            share(11 + i // 2, b, block(1, 0, 0), lax.rem(tile + (dy // 2) * (tiles // 2), tiles)).start()
+        partner = block(0, 0, 1)
+
+        @pl.when(i == 2)
+        def _():
+            for n, dy in enumerate((1, 3)):
+                landed(block(0, dy, 0))
+                share(4 + n, block(0, dy, 0), partner, tile).start()
+                share(6 + n, block(0, dy, 0), block(1, 0, 0), opposite).start()
+            share(8, block(0, 3 - 2 * core, 0), block(0, 1 + 2 * core, 0), tile).start()
+
+        @pl.when(jnp.logical_or(dc == 1, i > 5))
+        def _():
+            landed(b)
+
+        @pl.when(jnp.logical_and(dc == 0, i > 7))
+        def _():
+            share(7 + i // 2, b, partner, tile).start()
+
+        @pl.when(i == 6)
+        def _():
+            share(9, b, partner, tile).start()
+            share(10, b, block(1, 0, 0), opposite).start()
 
         total = None
         for c in range(slots // 8):
             build(b, c, c % 2)
             term = product(b, c, c % 2)
             total = term if total is None else total + term
+            if c == 0:
+                @pl.when(i > 1)
+                def _():
+                    deliver(i - 1).start()
 
         part[b, 0] = total[:, :128]
         part[b, 1] = total[:, 128:]
@@ -328,10 +346,6 @@
         def _():
             back[me, 0] = total[:, :128]
             back[me, 1] = total[:, 128:]
-
-        @pl.when(i > 1)
-        def _():
-            deliver(i - 1).start()
 
         return carry
 
@@ -371,7 +385,7 @@
     span, slots = nu + na, source_block.shape[1]
     rows = 2 * span + nu // 2 + na
     vmem = pl.BlockSpec(memory_space=pltpu.VMEM)
-    hbm = pl.BlockSpec(memory_space=pl.ANY)
+    hbm = pl.BlockSpec(memory_space=pltpu.HBM)
     dma = pltpu.SemaphoreType.DMA
     out = pl.pallas_call(
         kernel,
@@ -386,14 +400,15 @@
             pltpu.VMEM((16, slots // 8 * nu, 256), F32),
             pltpu.VMEM((16, 2, nu, 128), F32), pltpu.VMEM((16, 2, nu, 128), F32),
             pltpu.VMEM((16, 12, nu, 128), F32), pltpu.VMEM((12, 16 * na + 8, 128), F32),
-            pltpu.VMEM((2, 8 * nu, 256), BF16), pltpu.VMEM((2, 8 * nu, 256), BF16),
-            pltpu.VMEM((16, 8, 128), jnp.int32), pltpu.SMEM((16, 8, 128), jnp.int32),
+            pltpu.VMEM((2, 8 * nu, 256), F32),
+            pltpu.VMEM((16, 1, 128), jnp.int32), pltpu.SMEM((16, 1, 128), jnp.int32),
             dma((3,)), dma((15,)), dma((16,)), dma((8,)), dma((8,)), dma((8,)), dma((8,)),
             dma((15,)), dma((16,)), dma((15,)), dma((16,)), dma((15,)), dma((16,)), dma,
         ],
-        compiler_params=pltpu.CompilerParams(collective_id=0, has_side_effects=True, vmem_limit_bytes=56 << 20),
+        compiler_params=pltpu.CompilerParams(collective_id=0, has_side_effects=True, vmem_limit_bytes=24 << 20),
         name="galerkin",
-    )(solution_modes.reshape(-1, 128), coefficient_modes.reshape(-1, 128), coupling[0], source_block, expansion_index)
+    )(*(pltpu.with_memory_space_constraint(v, pltpu.HBM) for v in (
+        solution_modes.reshape(-1, 128), coefficient_modes.reshape(-1, 128), coupling[0])), source_block, expansion_index)
     return out.reshape(solution_modes.shape)
 
 

time: 51.7 us -> 49.2 us (0.952)
  Pallas kernels: 49.6 us -> 47.3 us
    pallas_call x1, Pallas kernels: 49.6 us -> 47.3 us  [on_device(): pl.pallas_call(kernel, out_shape=jax.ShapeDtypeStruct((nu * 32, 128), F32...]
    unnamed x1 -> x5, local copies, waits for them, and re-layouts: 1.87 us -> 1.47 us
where the time goes in v5:
time: 49.2 us; the launch traced here: 48.8 us
  Pallas kernels  47.3 us (96%)
  local copies, waits for them, and re-layouts  1.47 us (3%)
    pallas_call x1, Pallas kernels, on_device(): pl.pallas_call(kernel, out_shape=jax.ShapeDtypeStruct((nu * 32, 128), F32...  47.3 us
    unnamed x5, local copies, waits for them, and re-layouts  1.47 us

profile of v5, /device:TPU:7, one launch (start us, length us, event | category | flops | bytes accessed | tf_op | source)
XLA Modules:
  0.0 48.8 jit_solution(1739075693233133423)
XLA Ops:
  0.0 0.0 copy-start
  0.0 0.0 copy-start.1
  0.0 0.7 %copy-done = s32[1,32]{1,0:T(1,128)S(1)} copy-done((s32[1,32]{1,0:T(1,128)S(1)}, s32[1,32]{1,0:T(1,128)}, u32[]{:S(2)}) %copy-start) | copy-done | bytes 152
  0.7 0.0 copy-done.1
  0.7 47.3 %galerkin.1 = f32[1024,128]{1,0:T(8,128)S(1)} custom-call(f32[1024,128]{1,0:T(8,128)} %bitcast.5, f32[256,128]{1,0:T(8,128)} %bitcast.7, f32[32,32,32]{2,1,0:T(8,128)} %bitcast.6, s32[1,32]{1,0:T(1,128)S(1)} %copy-done, s32[1,32]{1,0:T(1,128)S(1)} %copy-done.1), custom_call_target="tpu_custom_call" | custom-call | tf_op jit(solution)/shard_map/galerkin/pallas_call | solution.py:390
  48.0 0.8 %copy.7 = f32[32,4,8,128]{3,2,1,0:T(8,128)} copy(f32[32,4,8,128]{3,2,1,0:T(8,128)S(1)} %bitcast.4) | data formatting | bytes 1048576
Async XLA Ops:
  0.0 0.7 %copy-start = (s32[1,32]{1,0:T(1,128)S(1)}, s32[1,32]{1,0:T(1,128)}, u32[]{:S(2)}) copy-start(s32[1,32]{1,0:T(1,128)} %sb_ref.1) | copy-start | bytes 388
  0.0 0.7 %copy-start.1 = (s32[1,32]{1,0:T(1,128)S(1)}, s32[1,32]{1,0:T(1,128)}, u32[]{:S(2)}) copy-start(s32[1,32]{1,0:T(1,128)} %ei_ref.1) | copy-start | bytes 388

commit v6 on v5

--- a/solution.py
+++ b/solution.py
@@ -122,7 +122,7 @@
 def kernel(u_hbm, a_hbm, c_hbm, sb_ref, ei_ref, out_ref,
            u_ref, a_ref, c_ref, pieces, got, up_out, down_out, from_down, from_up, held, part, back,
            delta, faces, mixed, index_v, index_s,
-           in_sem, p_send, p_recv, m_send, m_recv, q_send, q_recv, c_send, c_recv, o_send, o_recv, i_send, i_recv, own_sem):
+           in_sem, p_send, p_recv, m_send, m_recv, q_send, q_recv, c_send, c_recv, o_send, o_recv, i_send, i_recv, s_send, s_recv, own_sem):
     me, tile = lax.axis_index("modes"), lax.axis_index("tiles")
     tiles = lax.axis_size("tiles")
     has_up, has_down = tile < tiles - 1, tile > 0
@@ -138,16 +138,21 @@
              for i, (s, d) in enumerate(((u_hbm, u_ref), (a_hbm, a_ref), (c_hbm, c_ref)))]
     for load in loads:
         load.start()
-    opposite = lax.rem(tile + tiles // 2, tiles)
+    row = tiles // 2
+    opposite = lax.rem(tile + row, tiles)
+    x = lax.rem(tile, row)
+    beside = [tile - x + lax.rem(x + d, row) for d in range(1, row)]
     chips = ((0, 0), (0, 1), (0, 3), (1, 0), (0, 2), (1, 1), (1, 3), (1, 2))
     offsets = [(dz, dy, dc) for dz, dy in chips for dc in range(2)][1:]
-    barrier = greet([{"modes": block(*o)} for o in offsets] + [{"modes": block(1, 0, 0), "tiles": opposite}])
-
-    @pl.when(has_up)
+    barrier = greet([{"modes": block(*o)} for o in offsets] + [{"modes": block(1, 0, 0), "tiles": opposite}]
+                    + [{"tiles": t} for t in beside])
+    wrap_up, wrap_down = has_up & (x == row - 1), has_down & (x == 0)
+
+    @pl.when(wrap_up)
     def _():
         pl.semaphore_signal(barrier, inc=1, device_id={"tiles": tile + 1}, device_id_type=pl.DeviceIdType.MESH)
 
-    @pl.when(has_down)
+    @pl.when(wrap_down)
     def _():
         pl.semaphore_signal(barrier, inc=1, device_id={"tiles": tile - 1}, device_id_type=pl.DeviceIdType.MESH)
 
@@ -156,6 +161,8 @@
     loads[1].wait()
     cut(a_ref, pieces, na, nu, span)
     rims(pieces, nu, na)
+    loads[2].wait()
+    pack(c_ref, held, me)
     index_v[me] = jnp.zeros((1, 128), jnp.int32)
     index_v[me, :, pl.ds(0, slots)] = sb_ref[...]
     index_v[me, :, pl.ds(slots, slots)] = ei_ref[...]
@@ -168,21 +175,39 @@
     def _():
         from_up[...] = jnp.zeros(from_up.shape, F32)
 
-    pl.semaphore_wait(barrier, 16 + has_up.astype(jnp.int32) + has_down.astype(jnp.int32))
+    pl.semaphore_wait(barrier, 15 + row + wrap_up.astype(jnp.int32) + wrap_down.astype(jnp.int32))
 
     own = pltpu.make_async_copy(pieces.at[me + 1], got.at[me], own_sem)
     own.start()
-    sends = []
-    for i, o in enumerate(offsets):
-        copy = remote(pieces.at[block(*o) + 1], got.at[me], p_send.at[i], p_recv.at[me], modes=block(*o))
+    def share(i, which, modes, to):
+        return remote(held.at[which], held.at[which], c_send.at[i], c_recv.at[which], modes=modes, tiles=to)
+
+    def quarter(i, which, q, modes, to):
+        place = held.at[which, pl.ds(pl.multiple_of(nu * q, nu), nu)]
+        return remote(place, place, s_send.at[i], s_recv.at[which, q], modes=modes, tiles=to)
+
+    partner = block(0, 0, 1)
+    for i, dy in enumerate((1, 3, 2)):
+        quarter(i, me, x, block(0, dy, 0), tile).start()
+    share(0, me, block(1, 0, 0), opposite).start()
+    share(1, me, partner, tile).start()
+    sends = [remote(index_v.at[me], index_v.at[me], i_send.at[i], i_recv.at[me], modes=block(*o))
+             for i, o in enumerate(offsets)]
+    sends += [remote(pieces.at[block(*o) + 1], got.at[me], p_send.at[i], p_recv.at[me], modes=block(*o))
+              for i, o in enumerate(offsets)]
+    for copy in sends:
         copy.start()
-        sends.append(copy)
-    for i, o in enumerate(offsets):
-        copy = remote(index_v.at[me], index_v.at[me], i_send.at[i], i_recv.at[me], modes=block(*o))
-        copy.start()
-        sends.append(copy)
-    loads[2].wait()
-    pack(c_ref, held, me)
+    for n, dy in enumerate((1, 3, 2)):
+        which = block(0, dy, 0)
+        quarter(0, which, x, which, tile).wait_recv()
+        for i, to in enumerate(beside):
+            quarter(3 + 3 * n + i, which, x, me, to).start()
+    for n, dy in enumerate((1, 3, 2)):
+        which = block(0, dy, 0)
+        for to in beside:
+            quarter(0, which, lax.rem(to, row), me, to).wait_recv()
+        share(2 + n, which, block(1, 0, 0), opposite).start()
+        share(5 + n, which, partner, tile).start()
 
     def upward(g):
         return remote(up_out.at[g], from_down.at[g], m_send.at[g], m_recv.at[g], tiles=tile + 1)
@@ -212,13 +237,6 @@
         def _():
             downward(g).start()
 
-    def share(i, which, modes, to):
-        return remote(held.at[which], held.at[which], c_send.at[i], c_recv.at[which], modes=modes, tiles=to)
-
-    share(0, me, block(0, 1, 0), tile).start()
-    share(1, me, block(0, 3, 0), tile).start()
-    share(2, me, block(1, 0, 0), tile).start()
-    share(3, me, block(0, 0, 1), tile).start()
     for o in offsets:
         source = block(*o)
         remote(index_v.at[source], index_v.at[source], i_send.at[0], i_recv.at[source], modes=source).wait_recv()
@@ -290,67 +308,54 @@
         both = jnp.dot(jnp.concatenate([high, small], axis=0), w_high, preferred_element_type=F32)
         return (both[:nu] + both[nu:]) + jnp.dot(high, w_small, preferred_element_type=F32)
 
-    def number(i):
-        k = i // 2
-        r = (k % 4 + k // 4) % 4
-        return k // 4, r + (r // 2) * (1 - 2 * (r % 2)), i % 2
+    def number(k):
+        k = (k + 1) % 8
+        r = k % 4
+        return k // 4, r + (r // 2) * (1 - 2 * (r % 2))
 
     def landed(which):
-        share(0, which, block(0, 0, 1), tile).wait_recv()
-
-    def deliver(i):
-        b = block(*number(i))
-        return remote(part.at[b], back.at[me], o_send.at[i - 1], o_recv.at[me], modes=b)
-
-    def advance(i, carry):
-        dz, dy, dc = number(i)
-        b = block(dz, dy, dc)
-
-        partner = block(0, 0, 1)
-
-        @pl.when(i == 2)
-        def _():
-            for n, dy in enumerate((1, 3)):
-                landed(block(0, dy, 0))
-                share(4 + n, block(0, dy, 0), partner, tile).start()
-                share(6 + n, block(0, dy, 0), block(1, 0, 0), opposite).start()
-            share(8, block(0, 3 - 2 * core, 0), block(0, 1 + 2 * core, 0), tile).start()
-
-        @pl.when(jnp.logical_or(dc == 1, i > 5))
-        def _():
-            landed(b)
-
-        @pl.when(jnp.logical_and(dc == 0, i > 7))
-        def _():
-            share(7 + i // 2, b, partner, tile).start()
-
-        @pl.when(i == 6)
-        def _():
-            share(9, b, partner, tile).start()
-            share(10, b, block(1, 0, 0), opposite).start()
-
-        total = None
-        for c in range(slots // 8):
-            build(b, c, c % 2)
-            term = product(b, c, c % 2)
-            total = term if total is None else total + term
-            if c == 0:
-                @pl.when(i > 1)
-                def _():
-                    deliver(i - 1).start()
-
-        part[b, 0] = total[:, :128]
-        part[b, 1] = total[:, 128:]
-
-        @pl.when(i == 0)
-        def _():
-            back[me, 0] = total[:, :128]
-            back[me, 1] = total[:, 128:]
+        share(0, which, partner, tile).wait_recv()
+
+    def deliver(i, b):
+        return remote(part.at[b], back.at[me], o_send.at[i], o_recv.at[me], modes=b)
+
+    def advance(k, carry):
+        dz, dy = number(k)
+        ahead = block(*number(k + 1), 0)
+        own_block, other_block = block(dz, dy, 0), block(dz, dy, 1)
+
+        @pl.when(k > 0)
+        def _():
+            last = number(k + 7)
+            deliver(2 * k - 2, block(*last, 0)).start()
+            deliver(2 * k - 1, block(*last, 1)).start()
+
+        @pl.when((k > 1) & (k < 6))
+        def _():
+            landed(ahead)
+            share(6 + k, ahead, partner, tile).start()
+
+        landed(other_block)
+        totals = []
+        for h, b in enumerate((own_block, other_block)):
+            total = None
+            for c in range(slots // 8):
+                build(b, c, c % 2)
+                term = product(b, c, c % 2)
+                total = term if total is None else total + term
+            totals.append(total)
+            for t in range(2):
+                part[b, t] = total[:, 128 * t:128 * (t + 1)]
+
+        @pl.when(k == 7)
+        def _():
+            for t in range(2):
+                back[me, t] = totals[0][:, 128 * t:128 * (t + 1)]
 
         return carry
 
-    lax.fori_loop(0, 16, advance, 0)
-    deliver(15).start()
+    lax.fori_loop(0, 8, advance, 0)
+    deliver(14, partner).start()
 
     for dz, dy, dc in offsets:
         source = block(dz, dy, dc)
@@ -367,9 +372,11 @@
     lax.fori_loop(0, nu // 8, restore, 0)
     for copy in sends:
         copy.wait_send()
+    for i in range(12):
+        share(i, me, partner, tile).wait_send()
+        quarter(i, me, x, partner, tile).wait_send()
     for i in range(15):
-        share(i, me, block(0, 0, 1), tile).wait_send()
-        deliver(i + 1).wait_send()
+        deliver(i, partner).wait_send()
     for g in range(8):
         @pl.when(has_up)
         def _():
@@ -403,7 +410,7 @@
             pltpu.VMEM((2, 8 * nu, 256), F32),
             pltpu.VMEM((16, 1, 128), jnp.int32), pltpu.SMEM((16, 1, 128), jnp.int32),
             dma((3,)), dma((15,)), dma((16,)), dma((8,)), dma((8,)), dma((8,)), dma((8,)),
-            dma((15,)), dma((16,)), dma((15,)), dma((16,)), dma((15,)), dma((16,)), dma,
+            dma((12,)), dma((16,)), dma((15,)), dma((16,)), dma((15,)), dma((16,)), dma((12,)), dma((16, 4)), dma,
         ],
         compiler_params=pltpu.CompilerParams(collective_id=0, has_side_effects=True, vmem_limit_bytes=24 << 20),
         name="galerkin",

time: 49.2 us -> 45.2 us (0.919)
  Pallas kernels: 47.3 us -> 43.6 us
    pallas_call x1, Pallas kernels: 47.3 us -> 43.6 us  [on_device(): pl.pallas_call(kernel, out_shape=jax.ShapeDtypeStruct((nu * 32, 128), F32...]
where the time goes in v6:
time: 45.2 us; the launch traced here: 45.1 us
  Pallas kernels  43.6 us (96%)
  local copies, waits for them, and re-layouts  1.47 us (3%)
    pallas_call x1, Pallas kernels, on_device(): pl.pallas_call(kernel, out_shape=jax.ShapeDtypeStruct((nu * 32, 128), F32...  43.6 us
    unnamed x5, local copies, waits for them, and re-layouts  1.47 us

profile of v6, /device:TPU:7, one launch (start us, length us, event | category | flops | bytes accessed | tf_op | source)
XLA Modules:
  0.0 45.1 jit_solution(4151624441355670526)
XLA Ops:
  0.0 0.0 copy-start
  0.0 0.0 copy-start.1
  0.0 0.7 %copy-done = s32[1,32]{1,0:T(1,128)S(1)} copy-done((s32[1,32]{1,0:T(1,128)S(1)}, s32[1,32]{1,0:T(1,128)}, u32[]{:S(2)}) %copy-start) | copy-done | bytes 152
  0.7 0.0 copy-done.1
  0.7 43.6 %galerkin.1 = f32[1024,128]{1,0:T(8,128)S(1)} custom-call(f32[1024,128]{1,0:T(8,128)} %bitcast.5, f32[256,128]{1,0:T(8,128)} %bitcast.7, f32[32,32,32]{2,1,0:T(8,128)} %bitcast.6, s32[1,32]{1,0:T(1,128)S(1)} %copy-done, s32[1,32]{1,0:T(1,128)S(1)} %copy-done.1), custom_call_target="tpu_custom_call" | custom-call | tf_op jit(solution)/shard_map/galerkin/pallas_call | solution.py:397
  44.3 0.8 %copy.7 = f32[32,4,8,128]{3,2,1,0:T(8,128)} copy(f32[32,4,8,128]{3,2,1,0:T(8,128)S(1)} %bitcast.4) | data formatting | bytes 1048576
Async XLA Ops:
  0.0 0.7 %copy-start = (s32[1,32]{1,0:T(1,128)S(1)}, s32[1,32]{1,0:T(1,128)}, u32[]{:S(2)}) copy-start(s32[1,32]{1,0:T(1,128)} %sb_ref.1) | copy-start | bytes 388
  0.0 0.7 %copy-start.1 = (s32[1,32]{1,0:T(1,128)S(1)}, s32[1,32]{1,0:T(1,128)}, u32[]{:S(2)}) copy-start(s32[1,32]{1,0:T(1,128)} %ei_ref.1) | copy-start | bytes 388

commit v7 on v6

--- a/solution.py
+++ b/solution.py
@@ -77,37 +77,10 @@
             place = pl.ds(pl.multiple_of(span * t + first + 8 * m, 8), 8)
             rows = [value_ref[pl.ds(256 * m + 16 * t + i, 8, stride=32), :] for i in range(16)]
             for p, value in enumerate(transpose_blocks(rows)):
-                pieces[p + 1, place] = value
+                pieces[p, place] = value
         return carry
 
-    lax.fori_loop(0, count // 8, one, 0)
-
-
-def rims(pieces, nu, na):
-    span = nu + na
-    for q in (0, 17):
-        pieces[q, pl.ds(0, 2 * span)] = jnp.zeros((2 * span, 128), F32)
-
-    def one(p, carry):
-        zz = lanes((8, 128)) % 8
-
-        def rim(first, spots, base):
-            for (t, side), spot in spots:
-                value = pieces[p + 2 * side, pl.ds(span * t + first, 8)]
-                shift = (spot - (0 if side else 7)) % 128
-                base = jnp.where(zz == spot, kroll(value, shift), base)
-            return base
-
-        outer = (((0, 1), 7), ((1, 1), 6), ((0, 0), 0), ((1, 0), 1))
-        inner = (((0, 1), 5), ((1, 1), 4), ((0, 0), 2), ((1, 0), 3))
-        for m in range(nu // 16):
-            value = rim(8 * m, outer, jnp.zeros((8, 128), F32))
-            pieces[p + 1, pl.ds(2 * span + 8 * m, 8)] = rim(nu // 2 + 8 * m, inner, value)
-        for m in range(na // 8):
-            pieces[p + 1, pl.ds(2 * span + nu // 2 + 8 * m, 8)] = rim(nu + 8 * m, outer, jnp.zeros((8, 128), F32))
-        return carry
-
-    lax.fori_loop(0, 16, one, 0, unroll=2)
+    lax.fori_loop(0, count // 8, one, 0, unroll=2 if count > 8 else 1)
 
 
 def pack(c_ref, held, me):
@@ -119,13 +92,16 @@
                 held[me, pl.ds(n * q + 8 * m, 8), pl.ds(128 * h, 128)] = jnp.concatenate(parts, axis=1)
 
 
-def kernel(u_hbm, a_hbm, c_hbm, sb_ref, ei_ref, out_ref,
-           u_ref, a_ref, c_ref, pieces, got, up_out, down_out, from_down, from_up, held, part, back,
+def kernel(u_hbm, a_hbm, c_hbm, sb_hbm, ei_hbm, out_ref,
+           u_ref, a_ref, c_ref, sb_ref, ei_ref, pieces, got, up_out, down_out, from_down, from_up,
+           next_out, last_out, from_last, from_next, held, part, back,
            delta, faces, mixed, index_v, index_s,
-           in_sem, p_send, p_recv, m_send, m_recv, q_send, q_recv, c_send, c_recv, o_send, o_recv, i_send, i_recv, s_send, s_recv, own_sem):
+           in_sem, p_send, p_recv, m_send, m_recv, q_send, q_recv,
+           n_send, n_recv, l_send, l_recv, c_send, c_recv, o_send, o_recv, i_send, i_recv, s_send, s_recv, own_sem):
     me, tile = lax.axis_index("modes"), lax.axis_index("tiles")
     tiles = lax.axis_size("tiles")
     has_up, has_down = tile < tiles - 1, tile > 0
+    has_next, has_last = me < 15, me > 0
     z, y, core = me // 8, lax.rem(me // 2, 4), lax.rem(me, 2)
     nu, na = u_ref.shape[0] // 32, a_ref.shape[0] // 32
     span = nu + na
@@ -135,7 +111,7 @@
         return lax.rem(z + dz, 2) * 8 + lax.rem(y + dy, 4) * 2 + lax.rem(core + dc, 2)
 
     loads = [pltpu.make_async_copy(s, d, in_sem.at[i])
-             for i, (s, d) in enumerate(((u_hbm, u_ref), (a_hbm, a_ref), (c_hbm, c_ref)))]
+             for i, (s, d) in enumerate(((u_hbm, u_ref), (a_hbm, a_ref), (c_hbm, c_ref), (sb_hbm, sb_ref), (ei_hbm, ei_ref)))]
     for load in loads:
         load.start()
     row = tiles // 2
@@ -160,8 +136,8 @@
     cut(u_ref, pieces, nu, 0, span)
     loads[1].wait()
     cut(a_ref, pieces, na, nu, span)
-    rims(pieces, nu, na)
-    loads[2].wait()
+    for load in loads[2:]:
+        load.wait()
     pack(c_ref, held, me)
     index_v[me] = jnp.zeros((1, 128), jnp.int32)
     index_v[me, :, pl.ds(0, slots)] = sb_ref[...]
@@ -175,9 +151,17 @@
     def _():
         from_up[...] = jnp.zeros(from_up.shape, F32)
 
+    @pl.when(jnp.logical_not(has_last))
+    def _():
+        from_last[...] = jnp.zeros(from_last.shape, F32)
+
+    @pl.when(jnp.logical_not(has_next))
+    def _():
+        from_next[...] = jnp.zeros(from_next.shape, F32)
+
     pl.semaphore_wait(barrier, 15 + row + wrap_up.astype(jnp.int32) + wrap_down.astype(jnp.int32))
 
-    own = pltpu.make_async_copy(pieces.at[me + 1], got.at[me], own_sem)
+    own = pltpu.make_async_copy(pieces.at[me], got.at[me], own_sem)
     own.start()
     def share(i, which, modes, to):
         return remote(held.at[which], held.at[which], c_send.at[i], c_recv.at[which], modes=modes, tiles=to)
@@ -193,7 +177,7 @@
     share(1, me, partner, tile).start()
     sends = [remote(index_v.at[me], index_v.at[me], i_send.at[i], i_recv.at[me], modes=block(*o))
              for i, o in enumerate(offsets)]
-    sends += [remote(pieces.at[block(*o) + 1], got.at[me], p_send.at[i], p_recv.at[me], modes=block(*o))
+    sends += [remote(pieces.at[block(*o)], got.at[me], p_send.at[i], p_recv.at[me], modes=block(*o))
               for i, o in enumerate(offsets)]
     for copy in sends:
         copy.start()
@@ -202,20 +186,20 @@
         quarter(0, which, x, which, tile).wait_recv()
         for i, to in enumerate(beside):
             quarter(3 + 3 * n + i, which, x, me, to).start()
-    for n, dy in enumerate((1, 3, 2)):
-        which = block(0, dy, 0)
-        for to in beside:
-            quarter(0, which, lax.rem(to, row), me, to).wait_recv()
-        share(2 + n, which, block(1, 0, 0), opposite).start()
-        share(5 + n, which, partner, tile).start()
-
     def upward(g):
         return remote(up_out.at[g], from_down.at[g], m_send.at[g], m_recv.at[g], tiles=tile + 1)
 
     def downward(g):
         return remote(down_out.at[g], from_up.at[g], q_send.at[g], q_recv.at[g], tiles=tile - 1)
 
-    low = lanes((8, 128)) < 64
+    def onward(g):
+        return remote(next_out.at[g], from_last.at[g], n_send.at[g], n_recv.at[g], modes=me + 1)
+
+    def backward(g):
+        return remote(last_out.at[g], from_next.at[g], l_send.at[g], l_recv.at[g], modes=me - 1)
+
+    lane = lanes((8, 128))
+    low, zz = lane < 64, lane % 8
     own.wait()
     for dz, dy in chips:
         for dc in range(2):
@@ -226,8 +210,13 @@
         for m in range(span // 8):
             first = pl.ds(8 * m, 8)
             second = pl.ds(span + 8 * m, 8)
-            up_out[g, first] = jnp.where(low, kroll(got[2 * g, second], 64), got[2 * g + 1, second])
-            down_out[g, first] = jnp.where(low, got[2 * g, first], kroll(got[2 * g + 1, first], 64))
+            e0, e1, o0, o1 = got[2 * g, first], got[2 * g, second], got[2 * g + 1, first], got[2 * g + 1, second]
+            up_out[g, first] = jnp.where(low, kroll(e1, 64), o1)
+            down_out[g, first] = jnp.where(low, e0, kroll(o0, 64))
+            rim = jnp.where(zz == 2, kroll(o0, 123), kroll(o1, 124))
+            next_out[g, first] = jnp.where(zz == 0, kroll(e0, 121), jnp.where(zz == 1, kroll(e1, 122), rim))
+            rim = jnp.where(zz == 5, kroll(o0, 5), kroll(o1, 4))
+            last_out[g, first] = jnp.where(zz == 7, kroll(e0, 7), jnp.where(zz == 6, kroll(e1, 6), rim))
 
         @pl.when(has_up)
         def _():
@@ -236,6 +225,21 @@
         @pl.when(has_down)
         def _():
             downward(g).start()
+
+        @pl.when(has_next)
+        def _():
+            onward(g).start()
+
+        @pl.when(has_last)
+        def _():
+            backward(g).start()
+
+    for n, dy in enumerate((1, 3, 2)):
+        which = block(0, dy, 0)
+        for to in beside:
+            quarter(0, which, lax.rem(to, row), me, to).wait_recv()
+        share(2 + n, which, block(1, 0, 0), opposite).start()
+        share(5 + n, which, partner, tile).start()
 
     for o in offsets:
         source = block(*o)
@@ -255,25 +259,31 @@
         def _():
             remote(up_out.at[g], from_down.at[g], m_send.at[g], m_recv.at[g], tiles=tile - 1).wait_recv()
 
+        @pl.when(has_last)
+        def _():
+            remote(next_out.at[g], from_last.at[g], n_send.at[g], n_recv.at[g], modes=me - 1).wait_recv()
+
+        @pl.when(has_next)
+        def _():
+            remote(last_out.at[g], from_next.at[g], l_send.at[g], l_recv.at[g], modes=me + 1).wait_recv()
+
         for odd in range(2):
             j = 2 * g + odd
 
-            def tiles_of(first, rim, shifts):
-                minus, plus = from_down[g, pl.ds(first, 8)], from_up[g, pl.ds(first, 8)]
+            def tiles_of(first):
+                place = pl.ds(first, 8)
+                minus, plus = from_down[g, place], from_up[g, place]
                 minus, plus = (kroll(minus, 64), plus) if odd else (minus, kroll(plus, 64))
-                value = got[j, pl.ds(2 * span + rim, 8)]
-                below = [kroll(value, s % 128) if s else value for s in shifts[:2]]
-                above = [kroll(value, s % 128) if s else value for s in shifts[2:]]
-                return got[j, pl.ds(first, 8)], got[j, pl.ds(span + first, 8)], below, above, minus, plus
+                below, above = from_last[g, place], from_next[g, place]
+                below = [kroll(below, 128 - n) if n else below for n in (2 * odd, 2 * odd + 1)]
+                above = [kroll(above, n) if n else above for n in (2 * odd, 2 * odd + 1)]
+                return got[j, place], got[j, pl.ds(span + first, 8)], below, above, minus, plus
 
             for m in range(nu // 8):
-                lower = m < nu // 16
-                rim = 8 * m if lower else 8 * m - nu // 2
-                parts = tiles_of(8 * m, rim, (0, -1, 0, 1) if lower else (-2, -3, 2, 3))
-                for f, value in enumerate(face_tiles(difference, *parts)):
+                for f, value in enumerate(face_tiles(difference, *tiles_of(8 * m))):
                     delta[j, f, pl.ds(8 * m, 8)] = value
             place = pl.ds(pl.multiple_of(8 * j, 8), 8)
-            for f, value in enumerate(face_tiles(mean, *tiles_of(nu, nu // 2, (0, -1, 0, 1)))):
+            for f, value in enumerate(face_tiles(mean, *tiles_of(nu))):
                 faces[f, place] = value
         return carry
 
@@ -369,7 +379,7 @@
                 out_ref[pl.ds(256 * m + 16 * t + i, 8, stride=32), :] = value
         return carry
 
-    lax.fori_loop(0, nu // 8, restore, 0)
+    lax.fori_loop(0, nu // 8, restore, 0, unroll=2)
     for copy in sends:
         copy.wait_send()
     for i in range(12):
@@ -386,36 +396,45 @@
         def _():
             downward(g).wait_send()
 
+        @pl.when(has_next)
+        def _():
+            onward(g).wait_send()
+
+        @pl.when(has_last)
+        def _():
+            backward(g).wait_send()
+
 
 def on_device(solution_modes, coefficient_modes, coupling, source_block, expansion_index):
     nu, na = solution_modes.shape[0], coefficient_modes.shape[0]
     span, slots = nu + na, source_block.shape[1]
-    rows = 2 * span + nu // 2 + na
+    rows = 2 * span
     vmem = pl.BlockSpec(memory_space=pltpu.VMEM)
     hbm = pl.BlockSpec(memory_space=pltpu.HBM)
     dma = pltpu.SemaphoreType.DMA
     out = pl.pallas_call(
         kernel,
         out_shape=jax.ShapeDtypeStruct((nu * 32, 128), F32),
-        in_specs=[hbm, hbm, hbm, vmem, vmem],
+        in_specs=[hbm] * 5,
         out_specs=vmem,
         scratch_shapes=[
             pltpu.VMEM((nu * 32, 128), F32), pltpu.VMEM((na * 32, 128), F32), pltpu.VMEM((slots, nu, nu), F32),
-            pltpu.VMEM((18, rows, 128), F32), pltpu.VMEM((16, rows, 128), F32),
-            pltpu.VMEM((8, span, 128), F32), pltpu.VMEM((8, span, 128), F32),
-            pltpu.VMEM((8, span, 128), F32), pltpu.VMEM((8, span, 128), F32),
+            pltpu.VMEM((1, slots), jnp.int32), pltpu.VMEM((1, slots), jnp.int32),
+            pltpu.VMEM((16, rows, 128), F32), pltpu.VMEM((16, rows, 128), F32),
+            *[pltpu.VMEM((8, span, 128), F32)] * 8,
             pltpu.VMEM((16, slots // 8 * nu, 256), F32),
             pltpu.VMEM((16, 2, nu, 128), F32), pltpu.VMEM((16, 2, nu, 128), F32),
             pltpu.VMEM((16, 12, nu, 128), F32), pltpu.VMEM((12, 16 * na + 8, 128), F32),
             pltpu.VMEM((2, 8 * nu, 256), F32),
             pltpu.VMEM((16, 1, 128), jnp.int32), pltpu.SMEM((16, 1, 128), jnp.int32),
-            dma((3,)), dma((15,)), dma((16,)), dma((8,)), dma((8,)), dma((8,)), dma((8,)),
+            dma((5,)), dma((15,)), dma((16,)), *[dma((8,))] * 8,
             dma((12,)), dma((16,)), dma((15,)), dma((16,)), dma((15,)), dma((16,)), dma((12,)), dma((16, 4)), dma,
         ],
         compiler_params=pltpu.CompilerParams(collective_id=0, has_side_effects=True, vmem_limit_bytes=24 << 20),
         name="galerkin",
     )(*(pltpu.with_memory_space_constraint(v, pltpu.HBM) for v in (
-        solution_modes.reshape(-1, 128), coefficient_modes.reshape(-1, 128), coupling[0])), source_block, expansion_index)
+        solution_modes.reshape(-1, 128), coefficient_modes.reshape(-1, 128), coupling[0],
+        source_block, expansion_index)))
     return out.reshape(solution_modes.shape)
 
 

time: 45.2 us -> 41.8 us (0.925)
  Pallas kernels: 43.6 us -> 40.9 us
  local copies, waits for them, and re-layouts: 1.47 us -> 0.8 us
    pallas_call x1, Pallas kernels: 43.6 us -> 40.9 us  [on_device(): pl.pallas_call(kernel, out_shape=jax.ShapeDtypeStruct((nu * 32, 128), F32...]
    unnamed x5 -> x1, local copies, waits for them, and re-layouts: 1.47 us -> 0.8 us
where the time goes in v7:
time: 41.8 us; the launch traced here: 41.7 us
  Pallas kernels  40.9 us (98%)
  local copies, waits for them, and re-layouts  0.8 us (2%)
    pallas_call x1, Pallas kernels, on_device(): pl.pallas_call(kernel, out_shape=jax.ShapeDtypeStruct((nu * 32, 128), F32...  40.9 us

profile of v7, /device:TPU:7, one launch (start us, length us, event | category | flops | bytes accessed | tf_op | source)
XLA Modules:
  0.0 41.7 jit_solution(7066873217486910763)
XLA Ops:
  0.0 40.9 %galerkin.1 = f32[1024,128]{1,0:T(8,128)S(1)} custom-call(f32[1024,128]{1,0:T(8,128)} %bitcast.5, f32[256,128]{1,0:T(8,128)} %bitcast.7, f32[32,32,32]{2,1,0:T(8,128)} %bitcast.6, s32[1,32]{1,0:T(1,128)} %sb_hbm.1, s32[1,32]{1,0:T(1,128)} %ei_hbm.1), custom_call_target="tpu_custom_call" | custom-call | tf_op jit(solution)/shard_map/galerkin/pallas_call | solution.py:415
  40.9 0.8 %copy.7 = f32[32,4,8,128]{3,2,1,0:T(8,128)} copy(f32[32,4,8,128]{3,2,1,0:T(8,128)S(1)} %bitcast.4) | data formatting | bytes 1048576

commit v8 on v7

--- a/solution.py
+++ b/solution.py
@@ -26,12 +26,12 @@
     return pltpu.roll(value, shift, value.ndim - 1)
 
 
-def transpose_blocks(rows):
+def transpose_blocks(rows, steps=(1, 2, 4, 8)):
     lane = lanes(rows[0].shape)
-    for d in (1, 2, 4, 8):
+    for d in steps:
         keep = (lane // 8) & d == 0
         fresh = list(rows)
-        for i in range(16):
+        for i in range(len(rows)):
             if not i & d:
                 fresh[i] = jnp.where(keep, rows[i], kroll(rows[i + d], 8 * d))
                 fresh[i + d] = jnp.where(keep, kroll(rows[i], 128 - 8 * d), rows[i + d])
@@ -52,23 +52,27 @@
     return barrier
 
 
-def face_tiles(comb, x0, x1, below, above, r_minus, r_plus):
+def inner_faces(comb, x0, x1):
     lane = lanes(x0.shape)
-    zz, yy, low = lane % 8, (lane // 8) % 8, lane < 64
+    yy, low = (lane // 8) % 8, lane < 64
     zero = jnp.zeros_like(x0)
     r0, r1 = kroll(x0, 64), kroll(x1, 64)
-    yield comb(x0, jnp.where(low, r0, r1))
-    yield comb(x1, jnp.where(low, r1, r_plus))
-    yield comb(x0, jnp.where(low, r_minus, r0))
-    yield comb(x1, jnp.where(low, r0, r1))
-    for x in (x0, x1):
-        yield comb(x, jnp.where(yy < 7, kroll(x, 120), zero))
-    for x in (x0, x1):
-        yield comb(x, jnp.where(yy > 0, kroll(x, 8), zero))
-    for x, rim in zip((x0, x1), above):
-        yield comb(x, jnp.where(zz < 7, kroll(x, 127), rim))
-    for x, rim in zip((x0, x1), below):
-        yield comb(x, jnp.where(zz > 0, kroll(x, 1), rim))
+    swapped = jnp.where(low, r0, r1)
+    yield 0, comb(x0, swapped)
+    yield 3, comb(x1, swapped)
+    for t, value in enumerate((x0, x1)):
+        yield 4 + t, comb(value, jnp.where(yy < 7, kroll(value, 120), zero))
+        yield 6 + t, comb(value, jnp.where(yy > 0, kroll(value, 8), zero))
+
+
+def outer_faces(comb, x0, x1, below, above, r_minus, r_plus):
+    lane = lanes(x0.shape)
+    zz, low = lane % 8, lane < 64
+    yield 1, comb(x1, jnp.where(low, kroll(x1, 64), r_plus))
+    yield 2, comb(x0, jnp.where(low, r_minus, kroll(x0, 64)))
+    for t, value in enumerate((x0, x1)):
+        yield 8 + t, comb(value, jnp.where(zz < 7, kroll(value, 127), above[t]))
+        yield 10 + t, comb(value, jnp.where(zz > 0, kroll(value, 1), below[t]))
 
 
 def cut(value_ref, pieces, count, first, span):
@@ -80,7 +84,7 @@
                 pieces[p, place] = value
         return carry
 
-    lax.fori_loop(0, count // 8, one, 0, unroll=2 if count > 8 else 1)
+    lax.fori_loop(0, count // 8, one, 0, unroll=1)
 
 
 def pack(c_ref, held, me):
@@ -201,12 +205,26 @@
     lane = lanes((8, 128))
     low, zz = lane < 64, lane % 8
     own.wait()
-    for dz, dy in chips:
-        for dc in range(2):
-            if (dz, dy, dc) != (0, 0, 0):
-                source = block(dz, dy, dc)
-                remote(pieces.at[1], got.at[source], p_send.at[0], p_recv.at[source], modes=source).wait_recv()
-        g = block(dz, dy, 0) // 2
+
+    def pair_of(i):
+        r = i % 4
+        return block(i // 4, r + (r // 2) * (1 - 2 * (r % 2)), 0) // 2
+
+    def arrived(source):
+        remote(pieces.at[0], got.at[source], p_send.at[0], p_recv.at[source], modes=source).wait_recv()
+
+    def arrive(i, carry):
+        g = pair_of(i)
+
+        @pl.when(i == 0)
+        def _():
+            arrived(partner)
+
+        @pl.when(i > 0)
+        def _():
+            arrived(2 * g)
+            arrived(2 * g + 1)
+
         for m in range(span // 8):
             first = pl.ds(8 * m, 8)
             second = pl.ds(span + 8 * m, 8)
@@ -234,7 +252,19 @@
         def _():
             backward(g).start()
 
-    for n, dy in enumerate((1, 3, 2)):
+        for odd in range(2):
+            j = 2 * g + odd
+            for m in range(nu // 8):
+                place = pl.ds(8 * m, 8)
+                for f, value in inner_faces(difference, got[j, place], got[j, pl.ds(span + 8 * m, 8)]):
+                    delta[j, f, place] = value
+            place = pl.ds(pl.multiple_of(8 * j, 8), 8)
+            for f, value in inner_faces(mean, got[j, pl.ds(nu, 8)], got[j, pl.ds(span + nu, 8)]):
+                faces[f, place] = value
+        return carry
+
+    lax.fori_loop(0, 8, arrive, 0)
+    for n, dy in enumerate((2, 1, 3)):
         which = block(0, dy, 0)
         for to in beside:
             quarter(0, which, lax.rem(to, row), me, to).wait_recv()
@@ -248,8 +278,7 @@
     indices.start()
 
     def prepare(i, carry):
-        dz, r = i // 4, i % 4
-        g = block(dz, r + (r // 2) * (1 - 2 * (r % 2)), 0) // 2
+        g = pair_of(i)
 
         @pl.when(has_up)
         def _():
@@ -280,10 +309,10 @@
                 return got[j, place], got[j, pl.ds(span + first, 8)], below, above, minus, plus
 
             for m in range(nu // 8):
-                for f, value in enumerate(face_tiles(difference, *tiles_of(8 * m))):
+                for f, value in outer_faces(difference, *tiles_of(8 * m)):
                     delta[j, f, pl.ds(8 * m, 8)] = value
             place = pl.ds(pl.multiple_of(8 * j, 8), 8)
-            for f, value in enumerate(face_tiles(mean, *tiles_of(nu))):
+            for f, value in outer_faces(mean, *tiles_of(nu)):
                 faces[f, place] = value
         return carry
 
@@ -321,7 +350,8 @@
     def number(k):
         k = (k + 1) % 8
         r = k % 4
-        return k // 4, r + (r // 2) * (1 - 2 * (r % 2))
+        dy = r + (r // 2) * (1 - 2 * (r % 2))
+        return k // 4, (dy + (k // 4) * (6 - 2 * dy)) % 4
 
     def landed(which):
         share(0, which, partner, tile).wait_recv()
@@ -367,15 +397,27 @@
     lax.fori_loop(0, 8, advance, 0)
     deliver(14, partner).start()
 
-    for dz, dy, dc in offsets:
-        source = block(dz, dy, dc)
-        remote(part.at[0], back.at[source], o_send.at[0], o_recv.at[source], modes=source).wait_recv()
+    for dz in range(2):
+        for o in offsets:
+            if o[0] == dz:
+                remote(part.at[0], back.at[block(*o)], o_send.at[0], o_recv.at[block(*o)], modes=block(*o)).wait_recv()
+        base = 8 * lax.rem(z + dz, 2)
+
+        def gather(m, carry):
+            place = pl.ds(pl.multiple_of(8 * m, 8), 8)
+            for t in range(2):
+                rows = [back[base + p, t, place] for p in range(8)]
+                for p, value in enumerate(transpose_blocks(rows, (1, 2, 4))):
+                    back[base + p, t, place] = value
+            return carry
+
+        lax.fori_loop(0, nu // 8, gather, 0)
 
     def restore(m, carry):
         place = pl.ds(pl.multiple_of(8 * m, 8), 8)
         for t in range(2):
             rows = [back[p, t, place] for p in range(16)]
-            for i, value in enumerate(transpose_blocks(rows)):
+            for i, value in enumerate(transpose_blocks(rows, (8,))):
                 out_ref[pl.ds(256 * m + 16 * t + i, 8, stride=32), :] = value
         return carry
 

time: 41.8 us -> 44.6 us (1.067)
  Pallas kernels: 40.9 us -> 43.7 us
    pallas_call x1, Pallas kernels: 40.9 us -> 43.7 us  [on_device(): pl.pallas_call(kernel, out_shape=jax.ShapeDtypeStruct((nu * 32, 128), F32...]
where the time goes in v8:
time: 44.6 us; the launch traced here: 44.5 us
  Pallas kernels  43.7 us (98%)
  local copies, waits for them, and re-layouts  0.8 us (2%)
    pallas_call x1, Pallas kernels, on_device(): pl.pallas_call(kernel, out_shape=jax.ShapeDtypeStruct((nu * 32, 128), F32...  43.7 us

profile of v8, /device:TPU:7, one launch (start us, length us, event | category | flops | bytes accessed | tf_op | source)
XLA Modules:
  0.0 44.5 jit_solution(16367118497140406698)
XLA Ops:
  0.0 43.7 %galerkin.1 = f32[1024,128]{1,0:T(8,128)S(1)} custom-call(f32[1024,128]{1,0:T(8,128)} %bitcast.5, f32[256,128]{1,0:T(8,128)} %bitcast.7, f32[32,32,32]{2,1,0:T(8,128)} %bitcast.6, s32[1,32]{1,0:T(1,128)} %sb_hbm.1, s32[1,32]{1,0:T(1,128)} %ei_hbm.1), custom_call_target="tpu_custom_call" | custom-call | tf_op jit(solution)/shard_map/galerkin/pallas_call | solution.py:457
  43.7 0.8 %copy.7 = f32[32,4,8,128]{3,2,1,0:T(8,128)} copy(f32[32,4,8,128]{3,2,1,0:T(8,128)S(1)} %bitcast.4) | data formatting | bytes 1048576

commit v9 on v7

--- a/solution.py
+++ b/solution.py
@@ -238,7 +238,7 @@
         which = block(0, dy, 0)
         for to in beside:
             quarter(0, which, lax.rem(to, row), me, to).wait_recv()
-        share(2 + n, which, block(1, 0, 0), opposite).start()
+        share(2 + n, which, block(1, 0, 0), tile if dy == 3 else opposite).start()
         share(5 + n, which, partner, tile).start()
 
     for o in offsets:

time: 41.8 us -> 40.6 us (0.971)
  Pallas kernels: 40.9 us -> 39.3 us
    pallas_call x1, Pallas kernels: 40.9 us -> 39.3 us  [on_device(): pl.pallas_call(kernel, out_shape=jax.ShapeDtypeStruct((nu * 32, 128), F32...]
where the time goes in v9:
time: 40.6 us; the launch traced here: 40.1 us
  Pallas kernels  39.3 us (97%)
  local copies, waits for them, and re-layouts  0.8 us (2%)
    pallas_call x1, Pallas kernels, on_device(): pl.pallas_call(kernel, out_shape=jax.ShapeDtypeStruct((nu * 32, 128), F32...  39.3 us

profile of v9, /device:TPU:7, one launch (start us, length us, event | category | flops | bytes accessed | tf_op | source)
XLA Modules:
  0.0 40.1 jit_solution(1474151271247592660)
XLA Ops:
  0.0 39.3 %galerkin.1 = f32[1024,128]{1,0:T(8,128)S(1)} custom-call(f32[1024,128]{1,0:T(8,128)} %bitcast.5, f32[256,128]{1,0:T(8,128)} %bitcast.7, f32[32,32,32]{2,1,0:T(8,128)} %bitcast.6, s32[1,32]{1,0:T(1,128)} %sb_hbm.1, s32[1,32]{1,0:T(1,128)} %ei_hbm.1), custom_call_target="tpu_custom_call" | custom-call | tf_op jit(solution)/shard_map/galerkin/pallas_call | solution.py:415
  39.3 0.8 %copy.7 = f32[32,4,8,128]{3,2,1,0:T(8,128)} copy(f32[32,4,8,128]{3,2,1,0:T(8,128)S(1)} %bitcast.4) | data formatting | bytes 1048576

commit v10 on v9

--- a/solution.py
+++ b/solution.py
@@ -367,6 +367,31 @@
     lax.fori_loop(0, 8, advance, 0)
     deliver(14, partner).start()
 
+    for copy in sends:
+        copy.wait_send()
+    for i in range(12):
+        share(i, me, partner, tile).wait_send()
+        quarter(i, me, x, partner, tile).wait_send()
+
+    def drained(g, carry):
+        @pl.when(has_up)
+        def _():
+            upward(g).wait_send()
+
+        @pl.when(has_down)
+        def _():
+            downward(g).wait_send()
+
+        @pl.when(has_next)
+        def _():
+            onward(g).wait_send()
+
+        @pl.when(has_last)
+        def _():
+            backward(g).wait_send()
+        return carry
+
+    lax.fori_loop(0, 8, drained, 0)
     for dz, dy, dc in offsets:
         source = block(dz, dy, dc)
         remote(part.at[0], back.at[source], o_send.at[0], o_recv.at[source], modes=source).wait_recv()
@@ -380,29 +405,8 @@
         return carry
 
     lax.fori_loop(0, nu // 8, restore, 0, unroll=2)
-    for copy in sends:
-        copy.wait_send()
-    for i in range(12):
-        share(i, me, partner, tile).wait_send()
-        quarter(i, me, x, partner, tile).wait_send()
     for i in range(15):
         deliver(i, partner).wait_send()
-    for g in range(8):
-        @pl.when(has_up)
-        def _():
-            upward(g).wait_send()
-
-        @pl.when(has_down)
-        def _():
-            downward(g).wait_send()
-
-        @pl.when(has_next)
-        def _():
-            onward(g).wait_send()
-
-        @pl.when(has_last)
-        def _():
-            backward(g).wait_send()
 
 
 def on_device(solution_modes, coefficient_modes, coupling, source_block, expansion_index):

time: 40.6 us -> 40.5 us (level)
  no operation moved by 1% of the time
where the time goes in v10:
time: 40.5 us; the launch traced here: 40 us
  Pallas kernels  39.2 us (97%)
  local copies, waits for them, and re-layouts  0.8 us (2%)
    pallas_call x1, Pallas kernels, on_device(): pl.pallas_call(kernel, out_shape=jax.ShapeDtypeStruct((nu * 32, 128), F32...  39.2 us

profile of v10, /device:TPU:7, one launch (start us, length us, event | category | flops | bytes accessed | tf_op | source)
XLA Modules:
  0.0 40.0 jit_solution(6087304552306755554)
XLA Ops:
  0.0 39.2 %galerkin.1 = f32[1024,128]{1,0:T(8,128)S(1)} custom-call(f32[1024,128]{1,0:T(8,128)} %bitcast.5, f32[256,128]{1,0:T(8,128)} %bitcast.7, f32[32,32,32]{2,1,0:T(8,128)} %bitcast.6, s32[1,32]{1,0:T(1,128)} %sb_hbm.1, s32[1,32]{1,0:T(1,128)} %ei_hbm.1), custom_call_target="tpu_custom_call" | custom-call | tf_op jit(solution)/shard_map/galerkin/pallas_call | solution.py:419
  39.2 0.8 %copy.7 = f32[32,4,8,128]{3,2,1,0:T(8,128)} copy(f32[32,4,8,128]{3,2,1,0:T(8,128)S(1)} %bitcast.4) | data formatting | bytes 1048576
